TPU v7x, 1024 devices: a whole 8x8x8 slice. The times are simulated.
1024 devices in a mesh: dx: 8 (over y), dy: 8 (over z), dz: 16 (over x, core).
Axes of the slice: x: 8, y: 8, z: 8, core: 2. Of those that a mesh axis runs over, the one named last changes fastest.
Arguments:
- gas_core: float32 [5, 8, 8, 131072], P(None, 'dx', 'dy', 'dz')
- gas_vel: float32 [3, 8, 8, 131072], P(None, 'dx', 'dy', 'dz'), may hold values from -6 to 6
- gas_energy: float32 [8, 8, 131072], P('dx', 'dy', 'dz'), may hold values from 0.5 to 2
- cell_pairs: int32 [2, 8, 8, 256], P(None, 'dx', 'dy', 'dz'), may hold values from 0 to 35, as said below
- bh_coord: float32 [3, 8, 8, 2048], P(None, 'dx', 'dy', 'dz')
- bh_vel: float32 [3, 8, 8, 2048], P(None, 'dx', 'dy', 'dz'), may hold values from -6 to 6
- bh_mass: float32 [8, 8, 2048], P('dx', 'dy', 'dz'), may hold values from 20 to 80
- bh_soft: float32 [8, 8, 2048], P('dx', 'dy', 'dz'), may hold values from 8 to 32
- mem_gas: int32 [8, 8, 49152], P('dx', 'dy', 'dz'), may hold values from 0 to 8191
- mem_slot: int32 [8, 8, 49152], P('dx', 'dy', 'dz'), may hold values from 0 to 127, as said below
- send_count: int32 [8, 8, 2048], P('dx', 'dy', 'dz'), may hold values from 0 to 24, as said below
Outputs:
- density: float32 [8, 8, 131072], P('dx', 'dy', 'dz')
- gas_update: float32 [2, 8, 8, 131072], P(None, 'dx', 'dy', 'dz')
- bh_update: float32 [2, 8, 8, 2048], P(None, 'dx', 'dy', 'dz')
Inputs may be any that keep to these rules, and one draw needn't show every extreme that they name: `cell_pairs`: row 0 is a cell of the device and row 1 an extended cell at most 10 cells from it and never the same cell; the pairs of one device are distinct; every device lists (0, 9) and (15, 26). `mem_gas`: A particle may appear in several entries. `mem_slot`: the live entries of a block are ordered by slot; all live entries of one black hole come from a single device of its slab, whose domain holds the black hole, and they number 24 // 2 to 24. `send_count`: in every dx slab some blocks hold 24 live entries.
All inputs are finite; a program needn't handle non-finite values.
Results may differ from a plain program's by a relative error of at most 0.0003.
Values sent between devices are 32-bit elements; how exact they have to be, the bound alone decides.
No kernel may reach another device: no remote copies, remote signals or barrier semaphores. Data moves between devices by JAX's collectives and lax.ppermute only.
A program may use at most 64 MiB of HBM per device.

v0:
```python
import math

import jax
import jax.numpy as jnp
from jax import lax
from jax.sharding import PartitionSpec as P

CELL = 512
CPD = 16
BND = 10
NPAIR = 16
CAP = 24


kernel_norm = 21.0 / (2.0 * math.pi)
face_width = 32.0
cell_height = 0.5
bondi_coef = 0.04
edd_coef = 0.25
step_dt = 0.05
feed_coef = 20.0
heat_coef = 10.0 / 9.0


def with_halo(cells, sides, width):
    for axis, dim in sides:
        count = lax.axis_size(axis)
        head = lax.slice_in_dim(cells, 0, width, axis=dim)
        tail = lax.slice_in_dim(cells, cells.shape[dim] - width, cells.shape[dim], axis=dim)
        cells = jnp.concatenate(
            [
                lax.ppermute(tail, axis, [(i, (i + 1) % count) for i in range(count)]),
                cells,
                lax.ppermute(head, axis, [((i + 1) % count, i) for i in range(count)]),
            ],
            axis=dim,
        )
    return cells


def nearest(delta, length):
    half = 0.5 * length
    return jnp.where(delta > half, delta - length, jnp.where(delta < -half, delta + length, delta))


def block_density(rows, cols, z_length):
    delta_x = rows[0][:, None] - cols[0][None, :]
    delta_y = rows[1][:, None] - cols[1][None, :]
    delta_z = nearest(rows[2][:, None] - cols[2][None, :], z_length)
    smooth = 0.5 * (rows[4][:, None] + cols[4][None, :])
    ratio = jnp.sqrt(delta_x * delta_x + delta_y * delta_y + delta_z * delta_z) / smooth
    rest = jnp.maximum(1.0 - ratio, 0.0)
    kernel = (
        kernel_norm
        / (smooth * smooth * smooth)
        * (rest * rest)
        * (rest * rest)
        * (1.0 + 4.0 * ratio)
    )
    return jnp.sum(kernel * cols[3][None, :], axis=1)


def entry_terms(gas, hole, live, y_length, z_length):
    delta_x = gas[0] - hole[0]
    delta_y = nearest(gas[1] - hole[1], y_length)
    delta_z = nearest(gas[2] - hole[2], z_length)
    spread_sq = (delta_x * delta_x + delta_y * delta_y + delta_z * delta_z) / (hole[7] * hole[7])
    soft = 1.0 / (1.0 + spread_sq)
    weight = jnp.where(live, soft * soft, 0.0)
    mass_w = gas[6] * weight
    volume = weight * gas[6] / jnp.where(live, gas[8], 1.0)
    return jnp.stack(
        [mass_w, mass_w * gas[7], mass_w * gas[3], mass_w * gas[4], mass_w * gas[5], volume]
    )


def hole_rates(sums, hole_vel, hole_mass):
    mass_sum = sums[0]
    mean_heat = sums[1] / mass_sum
    drift = hole_vel - sums[2:5] / mass_sum[None]
    speed_sq = heat_coef * mean_heat + jnp.sum(drift * drift, axis=0)
    rho_hole = mass_sum / sums[5]
    bondi = bondi_coef * hole_mass * hole_mass * rho_hole / (speed_sq * jnp.sqrt(speed_sq))
    limit = edd_coef * hole_mass
    rate = jnp.minimum(bondi, limit)
    return (rate, rate / limit, rho_hole)


def send_group(blocks):
    return lax.all_to_all(blocks, ("dy", "dz"), split_axis=1, concat_axis=1, tiled=True)


def body(
    gas_core,
    gas_vel,
    gas_energy,
    cell_pairs,
    bh_coord,
    bh_vel,
    bh_mass,
    bh_soft,
    mem_gas,
    mem_slot,
    send_count,
):
    group = lax.axis_size("dy") * lax.axis_size("dz")
    holes = bh_mass.shape[2]
    local = CPD * CELL
    z_length = cell_height * CPD * lax.axis_size("dz")
    y_length = face_width * lax.axis_size("dy")
    core = gas_core.reshape(5, local)
    pairs = cell_pairs.reshape(2, NPAIR)
    wide = with_halo(gas_core, (("dz", 3),), BND * CELL)
    own = core.reshape(5, CPD, CELL)

    def own_cell(cell_id):
        block = lax.dynamic_index_in_dim(own, cell_id, 1, keepdims=False)
        return block_density(block, block, z_length)

    start = lax.map(own_cell, jnp.arange(CPD, dtype=jnp.int32))
    cells = wide.reshape(5, CPD + 2 * BND, CELL)

    def add_pair(step, total):
        home = pairs[0, step]
        other = pairs[1, step]
        rows = lax.dynamic_index_in_dim(cells, home + BND, 1, keepdims=False)
        cols = lax.dynamic_index_in_dim(cells, other, 1, keepdims=False)
        return total.at[home].add(block_density(rows, cols, z_length))

    rho = lax.fori_loop(0, NPAIR, add_pair, start).reshape(local)
    mass = core[3]
    heat = gas_energy.reshape(local)
    fields = jnp.concatenate(
        [core[0:3], gas_vel.reshape(3, local), core[3:4], heat[None], rho[None]], 0
    )
    index = mem_gas.reshape(group * CAP)
    picked = jnp.take(fields, index, axis=1)
    counts = send_count.reshape(group)
    live = (jnp.arange(CAP, dtype=jnp.int32)[None, :] < counts[:, None]).reshape(group * CAP)
    slot = mem_slot.reshape(group * CAP)
    hole_table = jnp.concatenate(
        [
            bh_coord.reshape(3, holes),
            bh_vel.reshape(3, holes),
            bh_mass.reshape(1, holes),
            bh_soft.reshape(1, holes),
        ],
        0,
    )
    slot_row = jnp.where(live, slot.astype(jnp.float32), -1.0)
    payload = jnp.concatenate([jnp.where(live[None], picked, 0.0), slot_row[None]], 0)
    arrived = send_group(payload.reshape(10, group, CAP)).reshape(10, group * CAP)
    alive = arrived[9] >= 0.0
    where_slot = jnp.maximum(arrived[9], 0.0).astype(jnp.int32)
    hole = jnp.take(hole_table, where_slot, axis=1)
    terms = entry_terms(arrived[:9], hole, alive, y_length, z_length)
    choose = (where_slot[:, None] == jnp.arange(holes, dtype=jnp.int32)[None, :]).astype(
        jnp.float32
    )
    sums = jnp.dot(terms, choose, precision=lax.Precision.HIGHEST)
    rate, ratio, rho_hole = hole_rates(sums, hole_table[3:6], hole_table[6])
    gain = step_dt * rate
    heat_gain = feed_coef * gain
    share = terms[5] / jnp.take(sums[5], where_slot)
    back = jnp.stack([jnp.take(gain, where_slot) * share, jnp.take(heat_gain, where_slot) * share])
    returned = send_group(back.reshape(2, group, CAP)).reshape(2, group * CAP)
    changes = jnp.zeros((2, local), jnp.float32).at[:, index].add(returned)
    gas_update = jnp.stack([mass - changes[0], heat + changes[1] / mass]).reshape(2, 1, 1, local)
    bh_update = jnp.stack([ratio, rho_hole]).reshape(2, 1, 1, holes)
    return (rho.reshape(1, 1, local), gas_update, bh_update)


def solution(mesh):
    in_specs = (
        P(None, "dx", "dy", "dz"),
        P(None, "dx", "dy", "dz"),
        P("dx", "dy", "dz"),
        P(None, "dx", "dy", "dz"),
        P(None, "dx", "dy", "dz"),
        P(None, "dx", "dy", "dz"),
        P("dx", "dy", "dz"),
        P("dx", "dy", "dz"),
        P("dx", "dy", "dz"),
        P("dx", "dy", "dz"),
        P("dx", "dy", "dz"),
    )
    out_specs = (P("dx", "dy", "dz"), P(None, "dx", "dy", "dz"), P(None, "dx", "dy", "dz"))
    return jax.shard_map(body, mesh=mesh, in_specs=in_specs, out_specs=out_specs, check_vma=False)
```

profile of v0, /device:TPU:1, one launch (start us, length us, event | category | flops | bytes accessed | tf_op | source)
XLA Modules:
  0.0 400.7 jit_solution(14123048556061028588)
XLA Ops:
  1.8 2.6 collective-permute-start
  4.4 11.5 %collective-permute-start.1 = (f32[5,1,1,5120]{3,2,1,0:T(1,128)S(1)}, f32[5,1,1,5120]{3,2,1,0:T(1,128)S(1)}, u32[]{:S(2)}, u32[]{:S(2)}) collective-permute-start(f32[5,1,1,5120]{3,2,1,0:T(1,128)S(1)} %get-tuple-element.270), channel_id=1, source_target_pairs={{1,0},{2,1},{3,2},{4,3},{5,4},{6,5},{7,6},{8,7},{9,8},{10,9},{11,1... | collective-permute-start | bytes 307208 | tf_op jit(solution)/shard_map/ppermute | solution.py:34
  23.2 67.5 %while.28 = (s32[]{:T(128)}, f32[16,512]{1,0:T(8,128)S(1)}, s32[16]{0:T(128)S(1)}, f32[5,16,512]{2,1,0:T(8,128)S(1)}, s32[]{:T(128)}, /*index=5*/s32[]{:T(128)}, s32[]{}, s32[]{:T(128)}, s32[]{}, s32[]{}, /*index=10*/s32[]{}) while((s32[]{:T(128)}, f32[16,512]{1,0:T(8,128)S(1)}, s32[16]{0:T(128)S(1)}, f32[5,16,512]{2,1,0:T(8,128)S(1)}, ...), condition=%wide.region_2.3_spmd, body=%wide.region_0.2_spmd.sunk | while | flops 7863817 | bytes 37099 | solution.py:120
  25.8 1.6 fusion.59
  30.0 1.6 fusion.59
  34.2 1.6 fusion.59
  38.4 1.6 fusion.59
  42.6 1.6 fusion.59
  46.9 1.6 fusion.59
  51.1 1.6 fusion.59
  55.3 1.6 fusion.59
  59.5 1.6 fusion.59
  63.7 1.6 fusion.59
  67.9 1.6 fusion.59
  72.2 1.6 fusion.59
  76.4 1.6 fusion.59
  92.1 141.4 %while.29 = (s32[]{:T(128)}, f32[16,512]{1,0:T(8,128)S(1)}, s32[2,16]{1,0:T(2,128)S(1)}, f32[5,36,512]{2,1,0:T(8,128)S(1)}, s32[]{:T(128)}, /*index=5*/s32[2]{0:...) while((s32[]{:T(128)}, f32[16,512]{1,0:T(8,128)S(1)}, ...), condition=%wide.region_6.7_spmd, body=%wide.region_3.6_spmd.sunk | while | flops 7864857 | bytes 67973 | solution.py:130
  98.7 1.6 fusion.60
  107.5 1.6 fusion.60
  116.3 1.6 fusion.60
  125.2 1.6 fusion.60
  134.0 1.6 fusion.60
  142.8 1.6 fusion.60
  151.7 1.6 fusion.60
  160.5 1.6 fusion.60
  169.3 1.6 fusion.60
  178.2 1.6 fusion.60
  187.0 1.6 fusion.60
  195.9 1.6 fusion.60
  204.7 1.6 fusion.60
  213.5 1.6 fusion.60
  222.4 1.6 fusion.60
  231.2 1.6 fusion.60
  233.8 2.6 copy.126
  236.5 10.3 %gather_fusion = f32[3072,9]{1,0:T(8,128)S(1)} fusion(f32[9,8192]{0,1:T(8,128)} %copy.126, s32[3072]{0:T(1024)S(1)} %broadcast_clamp_fusion.1), kind=kCustom, calls=%fused_computation.3 | custom fusion | bytes 233472 | tf_op jit(solution)/shard_map/jit(_take)/gather | solution.py:137
  249.3 13.3 %all-to-all-start = ((f32[128,1,240]{2,1,0:T(1,128)}), f32[128,1,240]{2,1,0:T(1,128)S(1)}, u32[]{:S(2)}, u32[]{:S(2)}) async-start(f32[128,1,240]{2,1,0:T(1,128)} %reshape.582), calls=%async_computation | async-start | bytes 262144 | tf_op jit(solution)/shard_map/all_to_all | solution.py:90
  263.4 11.9 %all-to-all-done = f32[128,1,240]{2,1,0:T(1,128)S(1)} async-done(((f32[128,1,240]{2,1,0:T(1,128)}), f32[128,1,240]{2,1,0:T(1,128)S(1)}, u32[]{:S(2)}, u32[]{:S(2)}) %all-to-all-start) | async-done | bytes 122912 | tf_op jit(solution)/shard_map/all_to_all | solution.py:90
  277.9 1.8 slice_reduce_fusion.4
  280.9 8.1 %gather_fusion.1 = f32[3072,8]{1,0:T(8,128)S(1)} fusion(f32[8,128]{0,1:T(8,128)S(1)} %copy.129, s32[3072]{0:T(1024)S(1)} %broadcast_clamp_fusion), kind=kCustom, calls=%fused_computation.4 | custom fusion | bytes 208896 | tf_op jit(solution)/shard_map/jit(_take)/gather | solution.py:155
  291.1 18.7 %gather_fusion.2 = f32[3072]{0:T(1024)S(1)} fusion(f32[128]{0:T(128)S(1)} %get-tuple-element.239, s32[3072]{0:T(1024)S(1)} %fusion.39), kind=kCustom, calls=%fused_computation.clone | custom fusion | bytes 36864 | tf_op jit(solution)/shard_map/jit(_take)/gather | solution.py:165
  309.8 18.7 %gather_fusion.4 = f32[3072]{0:T(1024)S(1)} fusion(f32[128]{0:T(128)S(1)} %get-tuple-element.240, s32[3072]{0:T(1024)S(1)} %fusion.39), kind=kCustom, calls=%fused_computation.2.clone | custom fusion | bytes 36864 | tf_op jit(solution)/shard_map/jit(_take)/gather | solution.py:165
  328.5 18.7 %gather_fusion.3 = f32[3072]{0:T(1024)S(1)} fusion(f32[128]{0:T(128)S(1)} %get-tuple-element.279, s32[3072]{0:T(1024)S(1)} %fusion.39), kind=kCustom, calls=%fused_computation.1.clone | custom fusion | bytes 36864 | tf_op jit(solution)/shard_map/jit(_take)/gather | solution.py:164
  348.1 5.6 %all-to-all-start.1 = ((f32[2,128,24]{2,0,1:T(2,128)}), f32[2,128,24]{2,0,1:T(2,128)S(1)}, u32[]{:S(2)}, u32[]{:S(2)}) async-start(f32[2,128,24]{2,0,1:T(2,128)} %copy.131), calls=%async_computation.1 | async-start | bytes 262144 | tf_op jit(solution)/shard_map/all_to_all | solution.py:90
  354.3 12.3 %all-to-all-done.1 = f32[2,128,24]{2,0,1:T(2,128)S(1)} async-done(((f32[2,128,24]{2,0,1:T(2,128)}), f32[2,128,24]{2,0,1:T(2,128)S(1)}, u32[]{:S(2)}, u32[]{:S(2)}) %all-to-all-start.1) | async-done | bytes 24608 | tf_op jit(solution)/shard_map/all_to_all | solution.py:90
  367.2 19.1 %scatter_custom_fusion = f32[2,8192]{0,1:T(8,128)} fusion(s32[3072]{0:T(1024)S(1)} %bitcast.187, f32[3072,2]{1,0:T(8,128)S(1)} %copy.133, f32[]{:T(128)} %constant.318.clone.1), kind=kCustom, calls=%fused_computation.55 | custom fusion | flops 6144 | bytes 65540 | tf_op jit(solution)/shard_map/scatter-add | solution.py:167
  386.2 7.9 %fusion.52 = (f32[1,8192]{0,1:T(8,128)}, f32[1,8192]{0,1:T(8,128)}) fusion(f32[2,8192]{0,1:T(8,128)} %scatter_custom_fusion), kind=kLoop, calls=%fused_computation.149 | loop fusion | bytes 131072 | tf_op jit(solution)/shard_map/slice | solution.py:168
  394.1 2.8 copy.142
  397.0 2.8 copy.143
  (232 shorter events, 70.0 us)
Async XLA Ops:
  0.6 91.5 %copy-start.4 = (s32[2]{0:T(128)S(1)}, s32[2]{0:T(128)}, u32[]{:S(2)}) copy-start(s32[2]{0:T(128)} %constant.298.clone.1) | copy-start | bytes 28
  0.6 90.1 %slice-start = ((f32[5,1,1,8192]{3,2,1,0:T(1,128)}), f32[3,1,1,8192]{3,2,1,0:T(1,128)S(1)}, s32[]{:S(2)}) async-start(f32[5,1,1,8192]{3,2,1,0:T(1,128)} %param.19), calls=%async_computation.2 | async-start | bytes 196608 | tf_op jit(solution)/shard_map/slice | solution.py:134
  0.7 90.3 %copy-start = (f32[5,1,1,8192]{3,2,1,0:T(1,128)S(1)}, f32[5,1,1,8192]{3,2,1,0:T(1,128)}, u32[]{:S(2)}) copy-start(f32[5,1,1,8192]{3,2,1,0:T(1,128)} %param.19) | copy-start | bytes 491524
  0.7 90.1 %copy-start.2 = (f32[3,1,1,8192]{3,2,1,0:T(1,128)S(1)}, f32[3,1,1,8192]{3,2,1,0:T(1,128)}, u32[]{:S(2)}) copy-start(f32[3,1,1,8192]{3,2,1,0:T(1,128)} %param.20) | copy-start | bytes 294916
  0.7 91.5 %copy-start.3 = (s32[2,1,1,16]{3,2,1,0:T(1,128)S(1)}, s32[2,1,1,16]{3,2,1,0:T(1,128)}, u32[]{:S(2)}) copy-start(s32[2,1,1,16]{3,2,1,0:T(1,128)} %param.22) | copy-start | bytes 388
  1.8 89.1 %collective-permute-start = (f32[5,1,1,5120]{3,2,1,0:T(1,128)S(1)}, f32[5,1,1,5120]{3,2,1,0:T(1,128)S(1)}, u32[]{:S(2)}, u32[]{:S(2)}) collective-permute-start(f32[5,1,1,5120]{3,2,1,0:T(1,128)S(1)} %get-tuple-element.269), channel_id=1, source_target_pairs={{0,1},{1,2},{2,3},{3,4},{4,5},{5,6},{6,7},{7,8},{8,9},{9,10},{10,1... | collective-permute-start | bytes 307208 | tf_op jit(solution)/shard_map/ppermute | solution.py:32
  4.4 86.5 %collective-permute-start.1 = (f32[5,1,1,5120]{3,2,1,0:T(1,128)S(1)}, f32[5,1,1,5120]{3,2,1,0:T(1,128)S(1)}, u32[]{:S(2)}, u32[]{:S(2)}) collective-permute-start(f32[5,1,1,5120]{3,2,1,0:T(1,128)S(1)} %get-tuple-element.270), channel_id=1, source_target_pairs={{1,0},{2,1},{3,2},{4,3},{5,4},{6,5},{7,6},{8,7},{9,8},{10,9},{11,1... | collective-permute-start | bytes 307208 | tf_op jit(solution)/shard_map/ppermute | solution.py:34
  23.2 210.4 %copy-start.1 = (f32[1,1,8192]{2,1,0:T(1,128)S(1)}, f32[1,1,8192]{2,1,0:T(1,128)}, u32[]{:S(2)}) copy-start(f32[1,1,8192]{2,1,0:T(1,128)} %param.21) | copy-start | bytes 98308
  246.8 15.8 %copy-start.5 = (f32[3,1,1,128]{3,2,1,0:T(1,128)S(1)}, f32[3,1,1,128]{3,2,1,0:T(1,128)}, u32[]{:S(2)}) copy-start(f32[3,1,1,128]{3,2,1,0:T(1,128)} %param.24) | copy-start | bytes 4612
  246.8 15.8 %copy-start.7 = (f32[3,1,1,128]{3,2,1,0:T(1,128)S(1)}, f32[3,1,1,128]{3,2,1,0:T(1,128)}, u32[]{:S(2)}) copy-start(f32[3,1,1,128]{3,2,1,0:T(1,128)} %param.23) | copy-start | bytes 4612
  246.8 15.8 %copy-start.6 = (f32[1,1,128]{2,1,0:T(1,128)S(1)}, f32[1,1,128]{2,1,0:T(1,128)}, u32[]{:S(2)}) copy-start(f32[1,1,128]{2,1,0:T(1,128)} %param.25) | copy-start | bytes 1540
  246.8 15.8 %copy-start.8 = (f32[1,1,128]{2,1,0:T(1,128)S(1)}, f32[1,1,128]{2,1,0:T(1,128)}, u32[]{:S(2)}) copy-start(f32[1,1,128]{2,1,0:T(1,128)} %param.26) | copy-start | bytes 1540
  249.3 26.0 %all-to-all-start = ((f32[128,1,240]{2,1,0:T(1,128)}), f32[128,1,240]{2,1,0:T(1,128)S(1)}, u32[]{:S(2)}, u32[]{:S(2)}) async-start(f32[128,1,240]{2,1,0:T(1,128)} %reshape.582), calls=%async_computation | async-start | bytes 262144 | tf_op jit(solution)/shard_map/all_to_all | solution.py:90
  348.1 18.4 %all-to-all-start.1 = ((f32[2,128,24]{2,0,1:T(2,128)}), f32[2,128,24]{2,0,1:T(2,128)S(1)}, u32[]{:S(2)}, u32[]{:S(2)}) async-start(f32[2,128,24]{2,0,1:T(2,128)} %copy.131), calls=%async_computation.1 | async-start | bytes 262144 | tf_op jit(solution)/shard_map/all_to_all | solution.py:90
where the time goes:
time: 403 us; the launch traced here: 401 us
  local copies, waits for them, and re-layouts  124 us (31%)
  loops' own time  115 us (29%)
  other arithmetic  103 us (26%)
  starting transfers between devices  33 us (8%)
  waiting for transfers between devices  24.1 us (6%)
    another operation x1, loops' own time, body(): rho = lax.fori_loop(0, NPAIR, add_pair, start).reshape(local)  83.4 us
    reduce_sum x32, other arithmetic, block_density(): return jnp.sum(kernel * cols[3][None, :], axis=1)  50.6 us
    another operation x1, loops' own time, body(): start = lax.map(own_cell, jnp.arange(CPD, dtype=jnp.int32))  31.6 us
    all_to_all x2, waiting for transfers between devices, send_group(): lax.all_to_all(blocks, ('dy', 'dz'), split_axis=1, concat_axis=1, tiled=T...  24.1 us
    another operation x32, other arithmetic  21.9 us
    scatter-add x1, other arithmetic, body(): changes = jnp.zeros((2, local), jnp.float32).at[:, index].add(returned)  19.1 us
    all_to_all x2, starting transfers between devices, send_group(): lax.all_to_all(blocks, ('dy', 'dz'), split_axis=1, concat_axis=1, tiled=T...  18.8 us
    gather x1, local copies, waits for them, and re-layouts, body(): jnp.take(gain, where_slot) * share  18.7 us
  transfers between devices with their start and end apart: 4, of which 2 were waited for; matrix products, arithmetic and copies ran while one was open for 11% of the time, Pallas kernels for 0%

commit v1 on v0

v1 whole, which is shorter than its diff:
```python
import functools
import math

import jax
import jax.numpy as jnp
from jax import lax
from jax.experimental import pallas as pl
from jax.experimental.pallas import tpu as pltpu
from jax.sharding import PartitionSpec as P

CELL = 512
CPD = 16
BND = 10
NPAIR = 16
CAP = 24
LANES = 128
GROUPS = CELL // LANES
ROWS = CPD * GROUPS
REACH = BND * GROUPS
NEAR = 16
UNROLL = 16

kernel_norm = 21.0 / (2.0 * math.pi)
face_width = 32.0
cell_height = 0.5
bondi_coef = 0.04
edd_coef = 0.25
step_dt = 0.05
feed_coef = 20.0
heat_coef = 10.0 / 9.0
tiny = 1e-37


def vmem():
    return pl.BlockSpec(memory_space=pltpu.VMEM)


def nearest(delta, length):
    half = 0.5 * length
    return jnp.where(delta > half, delta - length, jnp.where(delta < -half, delta + length, delta))


def pair_term(p, q, wrap):
    dx = p[0] - q[0]
    dy = p[1] - q[1]
    dz = p[2] - q[2]
    if wrap is not None:
        dz = jnp.abs(dz)
        dz = jnp.minimum(dz, wrap - dz)
    dist_sq = jnp.maximum(dx * dx + dy * dy + dz * dz, tiny)
    smooth = p[3] + q[3]
    inverse = lax.rsqrt(smooth * smooth)
    rest = jnp.maximum(1.0 - (dist_sq * lax.rsqrt(dist_sq)) * inverse, 0.0)
    scaled = rest * inverse
    return (scaled * scaled) * (scaled * (rest * (1.25 - rest)))


def block_density(cols, rows, wrap):
    def step(turn, total):
        total = list(total)
        for inner in range(UNROLL):
            start = pl.multiple_of((turn * UNROLL + inner) * 8, 8)
            tile = cols[pl.ds(start, 8), :]
            q = [jnp.broadcast_to(tile[:, f : f + 1], (8, LANES)) for f in range(5)]
            for g in range(GROUPS):
                total[g] = total[g] + pair_term(rows[g], q, wrap) * q[4]
        return tuple(total)

    zero = jnp.zeros((8, LANES), jnp.float32)
    total = lax.fori_loop(0, CELL // 8 // UNROLL, step, (zero,) * GROUPS)
    summed = jnp.concatenate([jnp.sum(t, axis=0, keepdims=True) for t in total], axis=0)
    return summed * (4.0 * kernel_norm)


def cell_rows(cell):
    return pl.ds(pl.multiple_of(cell * GROUPS, GROUPS), GROUPS)


def load_cell(ref, cell):
    x, y, z, mass, smooth = [ref[f, cell_rows(cell), :] for f in range(5)]
    return [x, y, z, 0.5 * smooth, mass]


def fill_cols(cols, fields):
    for g in range(GROUPS):
        stack = [f[g : g + 1] for f in fields] + [jnp.zeros((3, LANES), jnp.float32)]
        cols[g * LANES : (g + 1) * LANES, 0:8] = jnp.concatenate(stack, axis=0).T


def spread_rows(fields):
    return [[jnp.broadcast_to(f[g : g + 1], (8, LANES)) for f in fields[:4]] for g in range(GROUPS)]


def span(z):
    return jnp.min(z), jnp.max(z)


def own_kernel(z_length, core_ref, out_ref, cols):
    def run(wrap):
        @pl.loop(0, CPD)
        def _(cell):
            fields = load_cell(core_ref, cell)
            fill_cols(cols, fields)
            out_ref[cell_rows(cell), :] = block_density(cols, spread_rows(fields), wrap)

    low, high = span(core_ref[2])
    near = high - low <= 0.5 * z_length
    pl.when(near)(lambda: run(None))
    pl.when(jnp.logical_not(near))(lambda: run(z_length))


def own_density(core, z_length):
    return pl.pallas_call(
        functools.partial(own_kernel, z_length),
        out_shape=jax.ShapeDtypeStruct((ROWS, LANES), jnp.float32),
        in_specs=[vmem()],
        out_specs=vmem(),
        scratch_shapes=[pltpu.VMEM((CELL, LANES), jnp.float32)],
        cost_estimate=pl.CostEstimate(flops=CPD * CELL * CELL * 26, bytes_accessed=200000, transcendentals=0),
        name="own_density",
    )(core)


def lane_take(values, lanes):
    return jnp.take_along_axis(values, lanes, axis=1, mode="promise_in_bounds")


def hole_rates(sums, hole_vel, hole_mass):
    mass_sum = sums[0]
    mean_heat = sums[1] / mass_sum
    drift = [v - s / mass_sum for v, s in zip(hole_vel, sums[2:5])]
    speed_sq = heat_coef * mean_heat + (drift[0] * drift[0] + drift[1] * drift[1] + drift[2] * drift[2])
    rho_hole = mass_sum / sums[5]
    bondi = bondi_coef * hole_mass * hole_mass * rho_hole / (speed_sq * jnp.sqrt(speed_sq))
    limit = edd_coef * hole_mass
    rate = jnp.minimum(bondi, limit)
    return rate, rate / limit, rho_hole


def feed_kernel(
    y_length,
    z_length,
    group,
    pairs_ref,
    core_ref,
    lower_ref,
    upper_ref,
    own_ref,
    vel_ref,
    energy_ref,
    gas_id_ref,
    slot_ref,
    count_ref,
    holes_ref,
    rho_ref,
    update_ref,
    message_ref,
    cells,
    cols,
):
    half = 0.5 * z_length
    low, high = span(core_ref[2])
    plain = high - low <= half
    edges = ((lower_ref, slice(ROWS - REACH, ROWS), 0), (upper_ref, slice(0, REACH), REACH + ROWS))
    for ref, part, at in edges:
        z = ref[2, part, :]
        edge_low, edge_high = span(z)
        above = edge_low - high > half
        below = low - edge_high > half
        inside = jnp.logical_and(edge_high - low <= half, high - edge_low <= half)
        plain = jnp.logical_and(plain, jnp.logical_or(inside, jnp.logical_or(above, below)))
        shift = jnp.where(above, -z_length, jnp.where(below, z_length, 0.0))
        for f in (0, 1, 3, 4):
            cells[f, at : at + REACH, :] = ref[f, part, :]
        cells[2, at : at + REACH, :] = z + shift
    for f in range(5):
        cells[f, REACH : REACH + ROWS, :] = core_ref[f]
    rho_ref[...] = own_ref[...]

    def run(wrap):
        @pl.loop(0, NPAIR)
        def _(step):
            home = pairs_ref[step]
            other = pairs_ref[NPAIR + step]
            fill_cols(cols, load_cell(cells, other))
            rows = spread_rows(load_cell(core_ref, home))
            rho_ref[cell_rows(home), :] += block_density(cols, rows, wrap)

    pl.when(plain)(lambda: run(None))

    @pl.when(jnp.logical_not(plain))
    def _():
        for ref, part, at in edges:
            cells[2, at : at + REACH, :] = ref[2, part, :]
        run(z_length)

    lane = lax.broadcasted_iota(jnp.int32, (8, LANES), 1)
    sub = lax.broadcasted_iota(jnp.int32, (8, LANES), 0)
    coded = gas_id_ref[...] * LANES + slot_ref[...]
    turned = []
    for v in range(CAP // 8):
        place = CAP * lane + (8 * v + sub)
        place_row, place_lane = place >> 7, place & (LANES - 1)
        piece = jnp.zeros((8, LANES), jnp.int32)
        for r in range(CAP):
            row = jnp.broadcast_to(coded[r : r + 1], (8, LANES))
            piece = jnp.where(place_row == r, lane_take(row, place_lane), piece)
        turned.append(piece)
    count = count_ref[...]
    live = [(8 * v + sub) < count for v in range(CAP // 8)]
    gas_row = [t >> 14 for t in turned]
    gas_lane = [(t >> 7) & (LANES - 1) for t in turned]
    slot = [t & (LANES - 1) for t in turned]

    sources = [(core_ref, 0), (core_ref, 1), (core_ref, 2)] + [(vel_ref, 0), (vel_ref, 1), (vel_ref, 2)]
    sources = sources + [(core_ref, 3), (energy_ref, None), (rho_ref, None)]
    blocks = CAP // 8

    def gather(turn, picked):
        picked = list(picked)
        for inner in range(4):
            r = turn * 4 + inner
            for f, (ref, plane) in enumerate(sources):
                line = ref[pl.ds(r, 1), :] if plane is None else ref[plane, pl.ds(r, 1), :]
                line = jnp.broadcast_to(line, (8, LANES))
                for v in range(blocks):
                    at = f * blocks + v
                    picked[at] = jnp.where(gas_row[v] == r, lane_take(line, gas_lane[v]), picked[at])
        return tuple(picked)

    zero = jnp.zeros((8, LANES), jnp.float32)
    picked = lax.fori_loop(0, ROWS // 4, gather, (zero,) * (9 * blocks))
    gas = [jnp.concatenate(picked[f * blocks : (f + 1) * blocks], axis=0) for f in range(9)]
    live = jnp.concatenate([l.astype(jnp.int32) for l in live], axis=0) > 0
    slot = jnp.concatenate(slot, axis=0)
    gas_row = jnp.concatenate(gas_row, axis=0)
    gas_lane = jnp.concatenate(gas_lane, axis=0)

    first = slot[0:1]
    second = jnp.max(jnp.where(live & (slot != first), slot, -1), axis=0, keepdims=True)
    is_first = live & (slot == first)
    is_second = live & (slot != first)

    two = jnp.concatenate([first, jnp.maximum(second, 0)] * (LANES // 2), axis=0)
    chosen = two.astype(jnp.float32).T.astype(jnp.int32)
    wide_lane = lax.broadcasted_iota(jnp.int32, (LANES, LANES), 1)
    held = jnp.zeros((LANES, LANES), jnp.float32)
    for f in range(8):
        table = holes_ref[pl.ds(f, group, stride=8), :]
        held = jnp.where((wide_lane >> 1) == f, lane_take(table, chosen), held)
    held = held.T
    hole_first = [held[2 * f : 2 * f + 1] for f in range(8)]
    hole_second = [held[2 * f + 1 : 2 * f + 2] for f in range(8)]
    hole = [jnp.where(is_first, a, b) for a, b in zip(hole_first, hole_second)]

    delta_x = gas[0] - hole[0]
    delta_y = nearest(gas[1] - hole[1], y_length)
    delta_z = nearest(gas[2] - hole[2], z_length)
    spread_sq = (delta_x * delta_x + delta_y * delta_y + delta_z * delta_z) / (hole[7] * hole[7])
    soft = 1.0 / (1.0 + spread_sq)
    weight = jnp.where(live, soft * soft, 0.0)
    mass_w = gas[6] * weight
    volume = mass_w / jnp.where(live, gas[8], 1.0)
    terms = [mass_w, mass_w * gas[7], mass_w * gas[3], mass_w * gas[4], mass_w * gas[5], volume]

    def settle(mine, held_by):
        sums = [jnp.sum(jnp.where(mine, t, 0.0), axis=0, keepdims=True) for t in terms]
        rate, ratio, rho_hole = hole_rates(sums, held_by[3:6], held_by[6])
        return step_dt * rate, sums[5], ratio, rho_hole

    gain_a, volume_a, ratio_a, rho_a = settle(is_first, hole_first)
    gain_b, volume_b, ratio_b, rho_b = settle(is_second, hole_second)
    lost = jnp.where(is_first, gain_a, gain_b) * (volume / jnp.where(is_first, volume_a, volume_b))
    lost = jnp.where(live, lost, 0.0)

    has_a = count > 0
    has_b = second >= 0
    lines = [
        jnp.where(has_a, first.astype(jnp.float32), -1.0),
        jnp.where(has_a, ratio_a, 0.0),
        jnp.where(has_a, rho_a, 0.0),
        second.astype(jnp.float32),
        jnp.where(has_b, ratio_b, 0.0),
        jnp.where(has_b, rho_b, 0.0),
        jnp.zeros((2, LANES), jnp.float32),
    ]
    message_ref[...] = jnp.concatenate(lines, axis=0)

    high = lost.astype(jnp.bfloat16).astype(jnp.float32)
    mid = (lost - high).astype(jnp.bfloat16).astype(jnp.float32)
    low = (lost - high) - mid
    tall = lax.broadcasted_iota(jnp.int32, (LANES, LANES), 0)
    total = jnp.zeros((ROWS, 3 * LANES), jnp.float32)
    for k in range(CAP):
        at_row = (tall[:ROWS] == gas_row[k : k + 1]).astype(jnp.float32).astype(jnp.bfloat16)
        at_lane = tall == gas_lane[k : k + 1]
        parts = [jnp.where(at_lane, part[k : k + 1], 0.0).astype(jnp.bfloat16) for part in (high, mid, low)]
        total = total + lax.dot_general(
            at_row,
            jnp.concatenate(parts, axis=0),
            (((1,), (1,)), ((), ())),
            preferred_element_type=jnp.float32,
        )
    taken = total[:, 0:LANES] + total[:, LANES : 2 * LANES] + total[:, 2 * LANES :]
    mass = core_ref[3]
    update_ref[0] = mass - taken
    update_ref[1] = energy_ref[...] + feed_coef * taken / mass


def feed(pairs, core, lower, upper, own, vel, energy, gas_id, slot, count, holes, y_length, z_length, group):
    smem = pl.BlockSpec(memory_space=pltpu.SMEM)
    return pl.pallas_call(
        functools.partial(feed_kernel, y_length, z_length, group),
        out_shape=(
            jax.ShapeDtypeStruct((ROWS, LANES), jnp.float32),
            jax.ShapeDtypeStruct((2, ROWS, LANES), jnp.float32),
            jax.ShapeDtypeStruct((8, LANES), jnp.float32),
        ),
        in_specs=[smem] + [vmem()] * 10,
        out_specs=(vmem(),) * 3,
        scratch_shapes=[
            pltpu.VMEM((5, 2 * REACH + ROWS, LANES), jnp.float32),
            pltpu.VMEM((CELL, LANES), jnp.float32),
        ],
        cost_estimate=pl.CostEstimate(flops=NPAIR * CELL * CELL * 26, bytes_accessed=2000000, transcendentals=0),
        name="feed",
    )(pairs, core, lower, upper, own, vel, energy, gas_id, slot, count, holes)


def settle_kernel(group, arrived_ref, out_ref):
    lane = lax.broadcasted_iota(jnp.int32, (group, LANES), 1).astype(jnp.float32)
    parts = [jnp.broadcast_to(arrived_ref[:, f : f + 1], (group, LANES)) for f in range(6)]
    at_first = lane == parts[0]
    at_second = lane == parts[3]
    for k in range(2):
        value = jnp.where(at_first, parts[1 + k], jnp.where(at_second, parts[4 + k], 0.0))
        out_ref[k] = jnp.sum(value, axis=0, keepdims=True)


def settle(arrived, group):
    return pl.pallas_call(
        functools.partial(settle_kernel, group),
        out_shape=jax.ShapeDtypeStruct((2, 1, LANES), jnp.float32),
        in_specs=[vmem()],
        out_specs=vmem(),
        name="settle",
    )(arrived)


def body(gas_core, gas_vel, gas_energy, cell_pairs, bh_coord, bh_vel, bh_mass, bh_soft, mem_gas, mem_slot, send_count):
    group = lax.axis_size("dy") * lax.axis_size("dz")
    deep = lax.axis_size("dz")
    z_length = cell_height * CPD * deep
    y_length = face_width * lax.axis_size("dy")
    core = gas_core.reshape(5, ROWS, LANES)
    lower = lax.ppermute(core, "dz", [(i, (i + 1) % deep) for i in range(deep)])
    upper = lax.ppermute(core, "dz", [((i + 1) % deep, i) for i in range(deep)])
    table = jnp.concatenate(
        [bh_coord.reshape(3, LANES), bh_vel.reshape(3, LANES), bh_mass.reshape(1, LANES), bh_soft.reshape(1, LANES)], 0
    )
    copies = jnp.broadcast_to(table[None], (group, 8, LANES))
    holes = lax.all_to_all(copies, ("dy", "dz"), split_axis=0, concat_axis=0, tiled=True).reshape(group * 8, LANES)
    own = own_density(core, z_length)
    rho, update, message = feed(
        cell_pairs.reshape(2 * NPAIR),
        core,
        lower,
        upper,
        own,
        gas_vel.reshape(3, ROWS, LANES),
        gas_energy.reshape(ROWS, LANES),
        mem_gas.reshape(CAP, LANES),
        mem_slot.reshape(CAP, LANES),
        send_count.reshape(1, LANES),
        holes,
        y_length,
        z_length,
        group,
    )
    arrived = lax.all_to_all(message.T, ("dy", "dz"), split_axis=0, concat_axis=0, tiled=True)
    bh_update = settle(arrived, group)
    return (
        rho.reshape(1, 1, CPD * CELL),
        update.reshape(2, 1, 1, CPD * CELL),
        bh_update.reshape(2, 1, 1, LANES),
    )


def solution(mesh):
    lead, plain = P(None, "dx", "dy", "dz"), P("dx", "dy", "dz")
    in_specs = (lead, lead, plain, lead, lead, lead, plain, plain, plain, plain, plain)
    return jax.shard_map(body, mesh=mesh, in_specs=in_specs, out_specs=(plain, lead, lead), check_vma=False)
```

time: 403 us -> 115 us (0.29)
  local copies, waits for them, and re-layouts: 124 us -> 4.97 us
  loops' own time: 115 us -> 0 us
  other arithmetic: 103 us -> 0.67 us
  Pallas kernels: 0 us -> 55.6 us
  blocking collectives: 0 us -> 26.5 us
  waiting for transfers between devices: 24.1 us -> 0.01 us
  starting transfers between devices: 33 us -> 26.2 us
    another operation x2 -> x0, loops' own time: 115 us -> none  [the longest x1 83.4 us: body(): rho = lax.fori_loop(0, NPAIR, add_pair, start).reshape(local)]
    gather x7 -> x0, local copies, waits for them, and re-layouts: 75.7 us -> none  [the longest x1 18.7 us: body(): jnp.take(gain, where_slot) * share]
    pallas_call x0 -> x3, Pallas kernels: none -> 55.6 us  [the longest x1 31.1 us: feed(): pl.pallas_call(functools.partial(feed_kernel, y_length, z_length, group),...]
    reduce_sum x33 -> x0, other arithmetic: 50.6 us -> none  [the longest x32 50.6 us: block_density(): return jnp.sum(kernel * cols[3][None, :], axis=1)]
    all_to_all x0 -> x1, blocking collectives: none -> 26.5 us  [body(): lax.all_to_all(message.T, ('dy', 'dz'), split_axis=0, concat_axis=0, tile...]
    all_to_all x2 -> x1, waiting for transfers between devices: 24.1 us -> 0.01 us  [body(): lax.all_to_all(copies, ('dy', 'dz'), split_axis=0, concat_axis=0, tiled=T...]
    another operation x34 -> x0, other arithmetic: 22.5 us -> none
    scatter-add x1 -> x0, other arithmetic: 19.1 us -> none  [body(): changes = jnp.zeros((2, local), jnp.float32).at[:, index].add(returned)]
  transfers between devices with their start and end apart: 4 -> 3, of which waited for: 2 -> 0; matrix products, arithmetic and copies ran while one was open for 11% -> 2% of each run, Pallas kernels for 0% -> 20%
where the time goes in v1:
time: 115 us
  Pallas kernels  55.6 us (48%)
  blocking collectives  26.5 us (23%)
  starting transfers between devices  26.2 us (23%)
  local copies, waits for them, and re-layouts  4.97 us (4%)
    pallas_call x1, Pallas kernels, feed(): pl.pallas_call(functools.partial(feed_kernel, y_length, z_length, group),...  31.1 us
    all_to_all x1, blocking collectives, body(): lax.all_to_all(message.T, ('dy', 'dz'), split_axis=0, concat_axis=0, tile...  26.5 us
    all_to_all x1, starting transfers between devices, body(): lax.all_to_all(copies, ('dy', 'dz'), split_axis=0, concat_axis=0, tiled=T...  24.6 us
    pallas_call x1, Pallas kernels, own_density(): pl.pallas_call(functools.partial(own_kernel, z_length), out_shape=jax.Sha...  23 us
    unnamed x16, local copies, waits for them, and re-layouts  2.77 us
  transfers between devices with their start and end apart: 3, of which 0 were waited for; matrix products, arithmetic and copies ran while one was open for 2% of the time, Pallas kernels for 20%

profile of v1, /device:TPU:1, one launch (start us, length us, event | category | flops | bytes accessed | tf_op | source)
XLA Modules:
  0.0 114.6 jit_solution(12410321582702276385)
XLA Ops:
  0.6 0.7 copy_bitcast_fusion
  1.3 0.0 copy-start.5
  1.3 0.0 copy-start.6
  1.3 0.7 copy-done.5
  2.0 0.0 copy-done.6
  2.0 0.8 broadcast_in_dim.2
  2.8 0.0 copy-start.1
  2.8 24.6 %all-to-all-start = ((f32[128,8,128]{2,1,0:T(8,128)}), f32[128,8,128]{2,1,0:T(8,128)S(1)}, u32[]{:S(2)}, u32[]{:S(2)}) async-start(f32[128,8,128]{2,1,0:T(8,128)} %broadcast_in_dim.2), calls=%async_computation | async-start | bytes 1048576 | tf_op jit(solution)/shard_map/all_to_all | solution.py:362
  27.4 0.0 copy-done.1
  27.4 0.0 copy-start.4
  27.4 1.6 %collective-permute-start = (f32[5,64,128]{2,1,0:T(8,128)S(1)}, f32[5,64,128]{2,1,0:T(8,128)S(1)}, u32[]{:S(2)}, u32[]{:S(2)}) collective-permute-start(f32[5,64,128]{2,1,0:T(8,128)S(1)} %bitcast.26), channel_id=1, source_target_pairs={{0,1},{1,2},{2,3},{3,4},{4,5},{5,6},{6,7},{7,8},{8,9},{9,10},{10,1... | collective-permute-start | bytes 491528 | tf_op jit(solution)/shard_map/ppermute | solution.py:356
  29.1 0.0 collective-permute-start.1
  29.1 0.5 broadcast.4
  29.6 0.0 copy-done.4
  29.6 0.7 reduce.3
  30.3 0.6 reshape.54.pairs_ref
  30.9 23.0 %own_density.1.own_ref = f32[64,128]{1,0:T(8,128)} custom-call(f32[5,64,128]{2,1,0:T(8,128)} %bitcast.24), custom_call_target="tpu_custom_call" | custom-call | flops 109051904 | bytes 200000 | tf_op jit(solution)/shard_map/own_density/pallas_call | solution.py:113
  53.8 0.0 collective-permute-done.lower_ref
  53.8 0.0 copy-start.2
  53.8 0.0 collective-permute-done.1.upper_ref
  53.8 0.0 copy-start.3
  53.8 0.0 all-to-all-done
  53.9 0.0 copy-start
  53.9 0.6 copy-done.2
  54.5 0.1 copy-done.3
  54.6 0.2 copy-done
  54.7 31.1 %feed.1 = (f32[64,128]{1,0:T(8,128)}, f32[2,64,128]{2,1,0:T(8,128)}, f32[8,128]{1,0:T(8,128)}) custom-call(s32[32]{0:T(128)} %reshape.54.pairs_ref, f32[5,64,128]{2,1,0:T(8,128)} %bitcast.25, f32[5,64,128]{2,1,0:T(8,128)} %copy-done.2, f32[5,64,128]{2,1,0:T(8,128)} %copy-done.3, f32[64,128]{1,0:T(8,128)} %own_density.1.own_ref, f32[3,64,128]{2,1,0:T(8,128)} %bitcast.28, ...), custom_call_target="tpu_custom_call" | custom-call | flops 109051904 | bytes 2000000 | tf_op jit(solution)/shard_map/feed/pallas_call | solution.py:312
  85.8 0.8 copy.17
  86.6 26.5 %all_to_all.16 = f32[128,1,8]{2,1,0:T(1,128)} all-to-all(f32[128,1,8]{2,1,0:T(1,128)S(1)} %copy.17), channel_id=1, replica_groups=mesh['dx'=8,'dy'=8,'dz'=16] {'dy','dz'}, dimensions={0} | all-to-all | bytes 8192 | tf_op jit(solution)/shard_map/all_to_all | solution.py:380
  113.0 1.6 %settle.1 = f32[2,1,128]{2,1,0:T(1,128)} custom-call(f32[128,8]{1,0:T(8,128)} %bitcast.23), custom_call_target="tpu_custom_call" | custom-call | tf_op jit(solution)/shard_map/settle/pallas_call | solution.py:341
  (1 shorter events, 0.0 us)
Async XLA Ops:
  1.3 0.7 copy-start.5
  1.3 0.7 copy-start.6
  2.8 24.6 %copy-start.1 = (f32[5,1,1,8192]{3,2,1,0:T(1,128)S(1)}, f32[5,1,1,8192]{3,2,1,0:T(1,128)}, u32[]{:S(2)}) copy-start(f32[5,1,1,8192]{3,2,1,0:T(1,128)} %param.11) | copy-start | bytes 491524
  2.8 51.0 %all-to-all-start = ((f32[128,8,128]{2,1,0:T(8,128)}), f32[128,8,128]{2,1,0:T(8,128)S(1)}, u32[]{:S(2)}, u32[]{:S(2)}) async-start(f32[128,8,128]{2,1,0:T(8,128)} %broadcast_in_dim.2), calls=%async_computation | async-start | bytes 1048576 | tf_op jit(solution)/shard_map/all_to_all | solution.py:362
  27.4 2.2 %copy-start.4 = (s32[2,1,1,16]{3,2,1,0:T(1,128)S(1)}, s32[2,1,1,16]{3,2,1,0:T(1,128)}, u32[]{:S(2)}) copy-start(s32[2,1,1,16]{3,2,1,0:T(1,128)} %param.14) | copy-start | bytes 388
  27.4 26.4 %collective-permute-start = (f32[5,64,128]{2,1,0:T(8,128)S(1)}, f32[5,64,128]{2,1,0:T(8,128)S(1)}, u32[]{:S(2)}, u32[]{:S(2)}) collective-permute-start(f32[5,64,128]{2,1,0:T(8,128)S(1)} %bitcast.26), channel_id=1, source_target_pairs={{0,1},{1,2},{2,3},{3,4},{4,5},{5,6},{6,7},{7,8},{8,9},{9,10},{10,1... | collective-permute-start | bytes 491528 | tf_op jit(solution)/shard_map/ppermute | solution.py:356
  29.1 24.8 %collective-permute-start.1 = (f32[5,64,128]{2,1,0:T(8,128)S(1)}, f32[5,64,128]{2,1,0:T(8,128)S(1)}, u32[]{:S(2)}, u32[]{:S(2)}) collective-permute-start(f32[5,64,128]{2,1,0:T(8,128)S(1)} %bitcast.27), channel_id=1, source_target_pairs={{1,0},{2,1},{3,2},{4,3},{5,4},{6,5},{7,6},{8,7},{9,8},{10,9},{11,1... | collective-permute-start | bytes 491528 | tf_op jit(solution)/shard_map/ppermute | solution.py:357
  53.8 0.7 copy-start.2
  53.8 0.7 copy-start.3
  53.9 0.9 copy-start

commit v2 on v1

--- a/solution.py
+++ b/solution.py
@@ -17,7 +17,8 @@
 GROUPS = CELL // LANES
 ROWS = CPD * GROUPS
 REACH = BND * GROUPS
-NEAR = 16
+TILES = LANES // 8
+BINS = 32768.0
 UNROLL = 16
 
 kernel_norm = 21.0 / (2.0 * math.pi)
@@ -55,21 +56,71 @@
     return (scaled * scaled) * (scaled * (rest * (1.25 - rest)))
 
 
-def block_density(cols, rows, wrap):
+def load_cols(cols, tile):
+    return [cols[f, pl.ds(pl.multiple_of(tile * 8, 8), 8), :] for f in range(5)]
+
+
+def fold(parts):
+    return jnp.sum(parts, axis=0, keepdims=True)
+
+
+def dense_block(cols, rows, wrap):
     def step(turn, total):
         total = list(total)
-        for inner in range(UNROLL):
-            start = pl.multiple_of((turn * UNROLL + inner) * 8, 8)
-            tile = cols[pl.ds(start, 8), :]
-            q = [jnp.broadcast_to(tile[:, f : f + 1], (8, LANES)) for f in range(5)]
+        for inner in range(4):
+            q = load_cols(cols, turn * 4 + inner)
             for g in range(GROUPS):
                 total[g] = total[g] + pair_term(rows[g], q, wrap) * q[4]
         return tuple(total)
 
     zero = jnp.zeros((8, LANES), jnp.float32)
-    total = lax.fori_loop(0, CELL // 8 // UNROLL, step, (zero,) * GROUPS)
-    summed = jnp.concatenate([jnp.sum(t, axis=0, keepdims=True) for t in total], axis=0)
-    return summed * (4.0 * kernel_norm)
+    return lax.fori_loop(0, CELL // 32, step, (zero,) * GROUPS)
+
+
+def band_block(cols, rows):
+    def step(turn, total):
+        total = list(total)
+        for h in range(GROUPS):
+            for inner in range(UNROLL):
+                q = load_cols(cols, h * TILES + turn * UNROLL + inner)
+                for g in range(max(h - 1, 0), min(h + 2, GROUPS)):
+                    total[g] = total[g] + pair_term(rows[g], q, None) * q[4]
+        return tuple(total)
+
+    zero = jnp.zeros((8, LANES), jnp.float32)
+    return lax.fori_loop(0, TILES // UNROLL, step, (zero,) * GROUPS)
+
+
+def mirror_block(cols, rows, mirror):
+    def step(turn, total):
+        total = list(total)
+        for h in range(GROUPS):
+            for inner in range(UNROLL):
+                tile = turn * UNROLL + inner
+                q = load_cols(cols, h * TILES + tile)
+                total[h] = total[h] + pair_term(rows[h], q, None) * q[4]
+                if h + 1 < GROUPS:
+                    term = pair_term(rows[h + 1], q, None)
+                    total[h + 1] = total[h + 1] + term * q[4]
+                    mirror[pl.ds(pl.multiple_of((h * TILES + tile) * 8, 8), 8), :] = term * rows[h + 1][4]
+        return tuple(total)
+
+    zero = jnp.zeros((8, LANES), jnp.float32)
+    total = list(lax.fori_loop(0, TILES // UNROLL, step, (zero,) * GROUPS))
+    for h in range(GROUPS - 1):
+        part = mirror[h * LANES : (h + 1) * LANES, :].T
+        total[h] = total[h] + jnp.sum(part.reshape(TILES, 8, LANES), axis=0)
+    return total
+
+
+def corner_block(cols, row, h):
+    def step(turn, total):
+        for inner in range(4):
+            q = load_cols(cols, h * TILES + turn * 4 + inner)
+            total = total + pair_term(row, q, None) * q[4]
+        return total
+
+    return lax.fori_loop(0, TILES // 4, step, jnp.zeros((8, LANES), jnp.float32))
 
 
 def cell_rows(cell):
@@ -77,48 +128,214 @@
 
 
 def load_cell(ref, cell):
-    x, y, z, mass, smooth = [ref[f, cell_rows(cell), :] for f in range(5)]
-    return [x, y, z, 0.5 * smooth, mass]
+    return [ref[f, cell_rows(cell), :] for f in range(5)]
 
 
 def fill_cols(cols, fields):
     for g in range(GROUPS):
-        stack = [f[g : g + 1] for f in fields] + [jnp.zeros((3, LANES), jnp.float32)]
-        cols[g * LANES : (g + 1) * LANES, 0:8] = jnp.concatenate(stack, axis=0).T
+        for f in range(5):
+            cols[f, g * LANES : (g + 1) * LANES, :] = jnp.broadcast_to(fields[f][g : g + 1], (LANES, LANES)).T
 
 
 def spread_rows(fields):
-    return [[jnp.broadcast_to(f[g : g + 1], (8, LANES)) for f in fields[:4]] for g in range(GROUPS)]
+    return [[jnp.broadcast_to(f[g : g + 1], (8, LANES)) for f in fields] for g in range(GROUPS)]
+
+
+def put_total(out_ref, cell, total, add):
+    summed = jnp.concatenate([fold(t) for t in total], axis=0) * (4.0 * kernel_norm)
+    out_ref[cell_rows(cell), :] = out_ref[cell_rows(cell), :] + summed if add else summed
+
+
+def far_groups(p_stat, p_cell, q_stat, q_cell):
+    reach = p_stat[0, p_cell * GROUPS, 2] + q_stat[0, q_cell * GROUPS, 2]
+    reach = reach * 1.0001
+    found = []
+    for g in range(GROUPS):
+        for h in range(GROUPS):
+            if abs(g - h) >= 2:
+                p_low, p_high = p_stat[0, p_cell * GROUPS + g, 0], p_stat[0, p_cell * GROUPS + g, 1]
+                q_low, q_high = q_stat[0, q_cell * GROUPS + h, 0], q_stat[0, q_cell * GROUPS + h, 1]
+                near = jnp.logical_and(p_low - q_high <= reach, q_low - p_high <= reach)
+                found.append((g, h, near))
+    return found
+
+
+def run_corners(out_ref, cell, cols, rows, found):
+    for g, h, near in found:
+
+        @pl.when(near)
+        def _():
+            part = fold(corner_block(cols, rows[g], h)) * (4.0 * kernel_norm)
+            at = pl.ds(cell * GROUPS + g, 1)
+            out_ref[at, :] = out_ref[at, :] + part
 
 
 def span(z):
     return jnp.min(z), jnp.max(z)
 
 
-def own_kernel(z_length, core_ref, out_ref, cols):
-    def run(wrap):
+def by_group(ref, plane, g):
+    return ref[plane, pl.ds(g, CPD, stride=GROUPS), :]
+
+
+def ordered(keys):
+    depth = CELL // 8
+    lane = lax.broadcasted_iota(jnp.int32, (8, LANES), 1)
+    sub = lax.broadcasted_iota(jnp.int32, (8, LANES), 0)
+    lane_of = {64: 64, 128: 1, 256: 2}
+
+    def bit(step, block):
+        if step < 8:
+            return sub & step == 0
+        if step < 64:
+            return block * 8 & step == 0
+        return None if step >= CELL else lane & lane_of[step] == 0
+
+    def same(a, b):
+        if isinstance(a, bool) and isinstance(b, bool):
+            return a == b
+        if isinstance(a, bool):
+            a, b = b, a
+        if isinstance(b, bool):
+            return a if b else jnp.logical_not(a)
+        return jnp.logical_not(jnp.logical_xor(a, b))
+
+    size = 2
+    while size <= CELL:
+        gap = size // 2
+        while gap >= 1:
+            fresh = []
+            for k in range(len(keys)):
+                if gap >= 64:
+                    other = lane_take(keys[k], lane ^ lane_of[gap])
+                elif gap >= 8:
+                    other = keys[k ^ (gap // 8)]
+                else:
+                    down = pltpu.roll(keys[k], gap, 0)
+                    up = down if gap == 4 else pltpu.roll(keys[k], 8 - gap, 0)
+                    other = up if gap == 4 else jnp.where(sub & gap == 0, up, down)
+                rising = bit(size, k)
+                keep = same(bit(gap, k), True if rising is None else rising)
+                if isinstance(keep, bool):
+                    fresh.append(jnp.minimum(keys[k], other) if keep else jnp.maximum(keys[k], other))
+                else:
+                    fresh.append(jnp.where(keep, jnp.minimum(keys[k], other), jnp.maximum(keys[k], other)))
+            keys = fresh
+            gap //= 2
+        size *= 2
+    return keys
+
+
+def upright(rows):
+    half = rows.T
+    joined = jnp.concatenate([half[0:64], half[64:128]], axis=1)
+    return [joined[8 * k : 8 * k + 8] for k in range(8)]
+
+
+def flat(blocks):
+    joined = jnp.concatenate(blocks, axis=0)
+    return jnp.concatenate([joined[:, 0:64], joined[:, 64:128]], axis=0).T
+
+
+def remainder(key):
+    return key - jnp.floor(key * (1.0 / CELL)) * CELL
+
+
+def order_kernel(core_ref, out_ref, back_ref, spare):
+    lane = lax.broadcasted_iota(jnp.int32, (CPD, LANES), 1)
+    x = [by_group(core_ref, 0, g) for g in range(GROUPS)]
+    low = jnp.min(jnp.minimum(jnp.minimum(x[0], x[1]), jnp.minimum(x[2], x[3])), axis=1, keepdims=True)
+    high = jnp.max(jnp.maximum(jnp.maximum(x[0], x[1]), jnp.maximum(x[2], x[3])), axis=1, keepdims=True)
+    scale = (BINS - 1.0) / jnp.maximum(high - low, tiny)
+    for g in range(GROUPS):
+        bin_at = jnp.floor((x[g] - low) * scale)
+        bin_at = jnp.where(bin_at > 0.0, jnp.minimum(bin_at, BINS - 1.0), 0.0)
+        spare[pl.ds(g, CPD, stride=GROUPS), :] = bin_at * CELL + (lane + g * LANES).astype(jnp.float32)
+    keys = ordered(upright(spare[...]))
+    source = [remainder(k) for k in keys]
+    spare[...] = flat(source)
+    wide = lax.broadcasted_iota(jnp.int32, (8, LANES), 1)
+    deep = lax.broadcasted_iota(jnp.int32, (8, LANES), 0)
+    above = (wide & 3) * LANES + (wide >> 6) * 64 + deep
+    places = [(above + 8 * k).astype(jnp.float32) for k in range(8)]
+    back = ordered([s * CELL + p for s, p in zip(source, places)])
+    back_ref[...] = flat([remainder(k) for k in back]).astype(jnp.int32)
+    whole = [spare[pl.ds(g, CPD, stride=GROUPS), :].astype(jnp.int32) for g in range(GROUPS)]
+    for f, plane in enumerate((0, 1, 2, 4, 3)):
+        had = [by_group(core_ref, plane, g) for g in range(GROUPS)]
+        if plane == 4:
+            had = [0.5 * h for h in had]
+        now = []
+        for g in range(GROUPS):
+            group_at, lane_at = whole[g] >> 7, whole[g] & (LANES - 1)
+            value = lane_take(had[0], lane_at)
+            for other in range(1, GROUPS):
+                value = jnp.where(group_at == other, lane_take(had[other], lane_at), value)
+            now.append(value)
+            out_ref[f, pl.ds(g, CPD, stride=GROUPS), :] = value
+        if plane == 0:
+            lows = [jnp.min(v, axis=1, keepdims=True) for v in now]
+            highs = [jnp.max(v, axis=1, keepdims=True) for v in now]
+        if plane == 4:
+            tops = jnp.max(jnp.maximum(jnp.maximum(now[0], now[1]), jnp.maximum(now[2], now[3])), axis=1, keepdims=True)
+    for g in range(GROUPS):
+        stat = jnp.where(lane == 0, lows[g], jnp.where(lane == 1, highs[g], tops))
+        out_ref[5, pl.ds(g, CPD, stride=GROUPS), :] = stat
+
+
+def order(core):
+    return pl.pallas_call(
+        order_kernel,
+        out_shape=(
+            jax.ShapeDtypeStruct((6, ROWS, LANES), jnp.float32),
+            jax.ShapeDtypeStruct((ROWS, LANES), jnp.int32),
+        ),
+        in_specs=[vmem()],
+        out_specs=(vmem(), vmem()),
+        scratch_shapes=[pltpu.VMEM((ROWS, LANES), jnp.float32)],
+        cost_estimate=pl.CostEstimate(flops=3000000, bytes_accessed=400000, transcendentals=0),
+        name="order",
+    )(core)
+
+
+def own_kernel(z_length, stat_ref, core_ref, out_ref, cols, mirror):
+    low, high = span(core_ref[2])
+    plain = high - low <= 0.5 * z_length
+
+    @pl.when(plain)
+    def _():
         @pl.loop(0, CPD)
         def _(cell):
             fields = load_cell(core_ref, cell)
             fill_cols(cols, fields)
-            out_ref[cell_rows(cell), :] = block_density(cols, spread_rows(fields), wrap)
-
-    low, high = span(core_ref[2])
-    near = high - low <= 0.5 * z_length
-    pl.when(near)(lambda: run(None))
-    pl.when(jnp.logical_not(near))(lambda: run(z_length))
+            rows = spread_rows(fields)
+            put_total(out_ref, cell, mirror_block(cols, rows, mirror), False)
+            run_corners(out_ref, cell, cols, rows, far_groups(stat_ref, cell, stat_ref, cell))
+
+    @pl.when(jnp.logical_not(plain))
+    def _():
+        @pl.loop(0, CPD)
+        def _(cell):
+            fields = load_cell(core_ref, cell)
+            fill_cols(cols, fields)
+            put_total(out_ref, cell, dense_block(cols, spread_rows(fields), z_length), False)
+
+
+def stat_spec():
+    return pl.BlockSpec((1, ROWS, LANES), lambda i: (5, 0, 0), memory_space=pltpu.SMEM)
 
 
 def own_density(core, z_length):
     return pl.pallas_call(
         functools.partial(own_kernel, z_length),
         out_shape=jax.ShapeDtypeStruct((ROWS, LANES), jnp.float32),
-        in_specs=[vmem()],
+        in_specs=[stat_spec(), vmem()],
         out_specs=vmem(),
-        scratch_shapes=[pltpu.VMEM((CELL, LANES), jnp.float32)],
-        cost_estimate=pl.CostEstimate(flops=CPD * CELL * CELL * 26, bytes_accessed=200000, transcendentals=0),
+        scratch_shapes=[pltpu.VMEM((5, CELL, LANES), jnp.float32), pltpu.VMEM((CELL, LANES), jnp.float32)],
+        cost_estimate=pl.CostEstimate(flops=CPD * CELL * CELL * 12, bytes_accessed=400000, transcendentals=0),
+        grid=(1,),
         name="own_density",
-    )(core)
+    )(core, core)
 
 
 def lane_take(values, lanes):
@@ -142,10 +359,15 @@
     z_length,
     group,
     pairs_ref,
-    core_ref,
+    stat_ref,
+    lower_stat_ref,
+    upper_stat_ref,
+    sorted_ref,
     lower_ref,
     upper_ref,
     own_ref,
+    back_ref,
+    core_ref,
     vel_ref,
     energy_ref,
     gas_id_ref,
@@ -153,13 +375,15 @@
     count_ref,
     holes_ref,
     rho_ref,
-    update_ref,
     message_ref,
+    lost_ref,
+    gas_at_ref,
     cells,
     cols,
+    held_rho,
 ):
     half = 0.5 * z_length
-    low, high = span(core_ref[2])
+    low, high = span(sorted_ref[2])
     plain = high - low <= half
     edges = ((lower_ref, slice(ROWS - REACH, ROWS), 0), (upper_ref, slice(0, REACH), REACH + ROWS))
     for ref, part, at in edges:
@@ -174,25 +398,46 @@
             cells[f, at : at + REACH, :] = ref[f, part, :]
         cells[2, at : at + REACH, :] = z + shift
     for f in range(5):
-        cells[f, REACH : REACH + ROWS, :] = core_ref[f]
-    rho_ref[...] = own_ref[...]
-
-    def run(wrap):
+        cells[f, REACH : REACH + ROWS, :] = sorted_ref[f]
+    held_rho[...] = own_ref[...]
+
+    @pl.when(plain)
+    def _():
         @pl.loop(0, NPAIR)
         def _(step):
-            home = pairs_ref[step]
-            other = pairs_ref[NPAIR + step]
+            home = pairs_ref[0, step]
+            other = pairs_ref[1, step]
             fill_cols(cols, load_cell(cells, other))
-            rows = spread_rows(load_cell(core_ref, home))
-            rho_ref[cell_rows(home), :] += block_density(cols, rows, wrap)
-
-    pl.when(plain)(lambda: run(None))
+            rows = spread_rows(load_cell(sorted_ref, home))
+            put_total(held_rho, home, band_block(cols, rows), True)
+
+            def corners(q_stat, q_cell):
+                run_corners(held_rho, home, cols, rows, far_groups(stat_ref, home, q_stat, q_cell))
+
+            pl.when(other < BND)(lambda: corners(lower_stat_ref, other + (CPD - BND)))
+            pl.when(other >= BND + CPD)(lambda: corners(upper_stat_ref, other - (BND + CPD)))
+            pl.when(jnp.logical_and(other >= BND, other < BND + CPD))(lambda: corners(stat_ref, other - BND))
 
     @pl.when(jnp.logical_not(plain))
     def _():
         for ref, part, at in edges:
             cells[2, at : at + REACH, :] = ref[2, part, :]
-        run(z_length)
+
+        @pl.loop(0, NPAIR)
+        def _(step):
+            home = pairs_ref[0, step]
+            fill_cols(cols, load_cell(cells, pairs_ref[1, step]))
+            rows = spread_rows(load_cell(sorted_ref, home))
+            put_total(held_rho, home, dense_block(cols, rows, z_length), True)
+
+    for g in range(GROUPS):
+        back = back_ref[pl.ds(g, CPD, stride=GROUPS), :]
+        group_at, lane_at = back >> 7, back & (LANES - 1)
+        value = lane_take(held_rho[pl.ds(0, CPD, stride=GROUPS), :], lane_at)
+        for other in range(1, GROUPS):
+            moved = lane_take(held_rho[pl.ds(other, CPD, stride=GROUPS), :], lane_at)
+            value = jnp.where(group_at == other, moved, value)
+        rho_ref[pl.ds(g, CPD, stride=GROUPS), :] = value
 
     lane = lax.broadcasted_iota(jnp.int32, (8, LANES), 1)
     sub = lax.broadcasted_iota(jnp.int32, (8, LANES), 0)
@@ -284,8 +529,38 @@
         jnp.where(has_b, rho_b, 0.0),
         jnp.zeros((2, LANES), jnp.float32),
     ]
-    message_ref[...] = jnp.concatenate(lines, axis=0)
-
+    lines = jnp.concatenate(lines + [jnp.zeros((LANES - 8, LANES), jnp.float32)], axis=0)
+    message_ref[...] = lines.T[:, 0:8]
+    lost_ref[...] = lost
+    gas_at_ref[...] = gas_row * LANES + gas_lane
+
+
+def feed(pairs, ranked, lower, upper, own, back, core, vel, energy, gas_id, slot, count, holes, y_length, z_length, group):
+    smem = pl.BlockSpec(memory_space=pltpu.SMEM)
+    return pl.pallas_call(
+        functools.partial(feed_kernel, y_length, z_length, group),
+        out_shape=(
+            jax.ShapeDtypeStruct((ROWS, LANES), jnp.float32),
+            jax.ShapeDtypeStruct((group, 8), jnp.float32),
+            jax.ShapeDtypeStruct((CAP, LANES), jnp.float32),
+            jax.ShapeDtypeStruct((CAP, LANES), jnp.int32),
+        ),
+        in_specs=[smem] + [stat_spec()] * 3 + [vmem()] * 12,
+        out_specs=(vmem(),) * 4,
+        scratch_shapes=[
+            pltpu.VMEM((5, 2 * REACH + ROWS, LANES), jnp.float32),
+            pltpu.VMEM((5, CELL, LANES), jnp.float32),
+            pltpu.VMEM((ROWS, LANES), jnp.float32),
+        ],
+        cost_estimate=pl.CostEstimate(flops=NPAIR * CELL * CELL * 17, bytes_accessed=2000000, transcendentals=0),
+        grid=(1,),
+        name="feed",
+    )(pairs, ranked, lower, upper, ranked, lower, upper, own, back, core, vel, energy, gas_id, slot, count, holes)
+
+
+def apply_kernel(lost_ref, gas_at_ref, core_ref, energy_ref, update_ref):
+    lost = lost_ref[...]
+    gas_row, gas_lane = gas_at_ref[...] >> 7, gas_at_ref[...] & (LANES - 1)
     high = lost.astype(jnp.bfloat16).astype(jnp.float32)
     mid = (lost - high).astype(jnp.bfloat16).astype(jnp.float32)
     low = (lost - high) - mid
@@ -302,29 +577,22 @@
             preferred_element_type=jnp.float32,
         )
     taken = total[:, 0:LANES] + total[:, LANES : 2 * LANES] + total[:, 2 * LANES :]
-    mass = core_ref[3]
+    mass = core_ref[0]
     update_ref[0] = mass - taken
     update_ref[1] = energy_ref[...] + feed_coef * taken / mass
 
 
-def feed(pairs, core, lower, upper, own, vel, energy, gas_id, slot, count, holes, y_length, z_length, group):
-    smem = pl.BlockSpec(memory_space=pltpu.SMEM)
+def apply(lost, gas_at, core, energy):
+    mass_spec = pl.BlockSpec((1, ROWS, LANES), lambda i: (3, 0, 0), memory_space=pltpu.VMEM)
     return pl.pallas_call(
-        functools.partial(feed_kernel, y_length, z_length, group),
-        out_shape=(
-            jax.ShapeDtypeStruct((ROWS, LANES), jnp.float32),
-            jax.ShapeDtypeStruct((2, ROWS, LANES), jnp.float32),
-            jax.ShapeDtypeStruct((8, LANES), jnp.float32),
-        ),
-        in_specs=[smem] + [vmem()] * 10,
-        out_specs=(vmem(),) * 3,
-        scratch_shapes=[
-            pltpu.VMEM((5, 2 * REACH + ROWS, LANES), jnp.float32),
-            pltpu.VMEM((CELL, LANES), jnp.float32),
-        ],
-        cost_estimate=pl.CostEstimate(flops=NPAIR * CELL * CELL * 26, bytes_accessed=2000000, transcendentals=0),
-        name="feed",
-    )(pairs, core, lower, upper, own, vel, energy, gas_id, slot, count, holes)
+        apply_kernel,
+        out_shape=jax.ShapeDtypeStruct((2, ROWS, LANES), jnp.float32),
+        in_specs=[vmem(), vmem(), mass_spec, vmem()],
+        out_specs=vmem(),
+        cost_estimate=pl.CostEstimate(flops=1000000, bytes_accessed=100000, transcendentals=0),
+        grid=(1,),
+        name="apply",
+    )(lost, gas_at, core, energy)
 
 
 def settle_kernel(group, arrived_ref, out_ref):
@@ -353,22 +621,26 @@
     z_length = cell_height * CPD * deep
     y_length = face_width * lax.axis_size("dy")
     core = gas_core.reshape(5, ROWS, LANES)
-    lower = lax.ppermute(core, "dz", [(i, (i + 1) % deep) for i in range(deep)])
-    upper = lax.ppermute(core, "dz", [((i + 1) % deep, i) for i in range(deep)])
+    energy = gas_energy.reshape(ROWS, LANES)
+    ranked, back = order(core)
+    lower = lax.ppermute(ranked, "dz", [(i, (i + 1) % deep) for i in range(deep)])
+    upper = lax.ppermute(ranked, "dz", [((i + 1) % deep, i) for i in range(deep)])
     table = jnp.concatenate(
         [bh_coord.reshape(3, LANES), bh_vel.reshape(3, LANES), bh_mass.reshape(1, LANES), bh_soft.reshape(1, LANES)], 0
     )
     copies = jnp.broadcast_to(table[None], (group, 8, LANES))
     holes = lax.all_to_all(copies, ("dy", "dz"), split_axis=0, concat_axis=0, tiled=True).reshape(group * 8, LANES)
-    own = own_density(core, z_length)
-    rho, update, message = feed(
-        cell_pairs.reshape(2 * NPAIR),
-        core,
+    own = own_density(ranked, z_length)
+    rho, message, lost, gas_at = feed(
+        cell_pairs.reshape(2, NPAIR),
+        ranked,
         lower,
         upper,
         own,
+        back,
+        core,
         gas_vel.reshape(3, ROWS, LANES),
-        gas_energy.reshape(ROWS, LANES),
+        energy,
         mem_gas.reshape(CAP, LANES),
         mem_slot.reshape(CAP, LANES),
         send_count.reshape(1, LANES),
@@ -377,7 +649,8 @@
         z_length,
         group,
     )
-    arrived = lax.all_to_all(message.T, ("dy", "dz"), split_axis=0, concat_axis=0, tiled=True)
+    arrived = lax.all_to_all(message, ("dy", "dz"), split_axis=0, concat_axis=0, tiled=True)
+    update = apply(lost, gas_at, core, energy)
     bh_update = settle(arrived, group)
     return (
         rho.reshape(1, 1, CPD * CELL),

time: 115 us -> 93.5 us (0.81)
  blocking collectives: 26.5 us -> 0 us
  Pallas kernels: 55.6 us -> 40.2 us
  waiting for transfers between devices: 0.01 us -> 13 us
  starting transfers between devices: 26.2 us -> 35.4 us
  local copies, waits for them, and re-layouts: 4.97 us -> 3.61 us
    all_to_all x1 -> x0, blocking collectives: 26.5 us -> none  [body(): lax.all_to_all(message.T, ('dy', 'dz'), split_axis=0, concat_axis=0, tile...]
    pallas_call x1, Pallas kernels: 23 us -> 11.5 us  [own_density(): pl.pallas_call(functools.partial(own_kernel, z_length), out_shape=jax.Sha...]
    pallas_call x1, Pallas kernels: 31.1 us -> 21.1 us  [feed(): pl.pallas_call(functools.partial(feed_kernel, y_length, z_length, group),...]
    all_to_all x0 -> x1, starting transfers between devices: none -> 9.21 us  [body(): lax.all_to_all(message, ('dy', 'dz'), split_axis=0, concat_axis=0, tiled=...]
    all_to_all x0 -> x1, waiting for transfers between devices: none -> 8.84 us  [body(): lax.all_to_all(message, ('dy', 'dz'), split_axis=0, concat_axis=0, tiled=...]
    pallas_call x0 -> x2, Pallas kernels: none -> 6.05 us  [the longest x1 3.44 us: order(): pl.pallas_call(order_kernel, out_shape=(jax.ShapeDtypeStruct((6, ROWS, LA...]
    all_to_all x1, waiting for transfers between devices: 0.01 us -> 4.18 us  [body(): lax.all_to_all(copies, ('dy', 'dz'), split_axis=0, concat_axis=0, tiled=T...]
    unnamed x16 -> x13, local copies, waits for them, and re-layouts: 2.77 us -> 2.78 us
  transfers between devices with their start and end apart: 3 -> 4, of which waited for: 0 -> 2; matrix products, arithmetic and copies ran while one was open for 2% -> 0% of each run, Pallas kernels for 20% -> 19%
where the time goes in v2:
time: 93.5 us; the launch traced here: 92.9 us
  Pallas kernels  40.2 us (43%)
  starting transfers between devices  35.4 us (38%)
  waiting for transfers between devices  13 us (14%)
  local copies, waits for them, and re-layouts  3.61 us (4%)
    all_to_all x1, starting transfers between devices, body(): lax.all_to_all(copies, ('dy', 'dz'), split_axis=0, concat_axis=0, tiled=T...  24.4 us
    pallas_call x1, Pallas kernels, feed(): pl.pallas_call(functools.partial(feed_kernel, y_length, z_length, group),...  21.1 us
    pallas_call x1, Pallas kernels, own_density(): pl.pallas_call(functools.partial(own_kernel, z_length), out_shape=jax.Sha...  11.5 us
    all_to_all x1, starting transfers between devices, body(): lax.all_to_all(message, ('dy', 'dz'), split_axis=0, concat_axis=0, tiled=...  9.21 us
    all_to_all x1, waiting for transfers between devices, body(): lax.all_to_all(message, ('dy', 'dz'), split_axis=0, concat_axis=0, tiled=...  8.84 us
    all_to_all x1, waiting for transfers between devices, body(): lax.all_to_all(copies, ('dy', 'dz'), split_axis=0, concat_axis=0, tiled=T...  4.18 us
    pallas_call x1, Pallas kernels, order(): pl.pallas_call(order_kernel, out_shape=(jax.ShapeDtypeStruct((6, ROWS, LA...  3.44 us
    unnamed x13, local copies, waits for them, and re-layouts  2.78 us
  transfers between devices with their start and end apart: 4, of which 2 were waited for; matrix products, arithmetic and copies ran while one was open for 0% of the time, Pallas kernels for 19%

profile of v2, /device:TPU:1, one launch (start us, length us, event | category | flops | bytes accessed | tf_op | source)
XLA Modules:
  0.0 92.9 jit_solution(12813143817102996797)
XLA Ops:
  0.6 0.7 copy_bitcast_fusion
  1.3 0.0 copy-start.4
  1.3 0.0 copy-start.5
  1.3 0.7 copy-done.4
  2.0 0.0 copy-done.5
  2.0 0.8 broadcast_in_dim.2
  2.8 24.4 %all-to-all-start = ((f32[128,8,128]{2,1,0:T(8,128)}), f32[128,8,128]{2,1,0:T(8,128)S(1)}, u32[]{:S(2)}, u32[]{:S(2)}) async-start(f32[128,8,128]{2,1,0:T(8,128)} %broadcast_in_dim.2), calls=%async_computation | async-start | bytes 1048576 | tf_op jit(solution)/shard_map/all_to_all | solution.py:632
  27.3 3.4 %order.1 = (f32[6,64,128]{2,1,0:T(8,128)}, s32[64,128]{1,0:T(8,128)}) custom-call(f32[5,64,128]{2,1,0:T(8,128)} %bitcast.24), custom_call_target="tpu_custom_call" | custom-call | flops 3000000 | bytes 400000 | tf_op jit(solution)/shard_map/order/pallas_call | solution.py:287
  30.7 0.9 collective-permute-start.1
  31.6 0.9 collective-permute-start
  32.5 11.5 %own_density.1.own_ref = f32[64,128]{1,0:T(8,128)} custom-call(f32[6,64,128]{2,1,0:T(8,128)} %get-tuple-element.9.stat_ref.core_ref.sorted_ref, f32[6,64,128]{2,1,0:T(8,128)} %get-tuple-element.9.stat_ref.core_ref.sorted_ref), custom_call_target="tpu_custom_call" | custom-call | flops 50331648 | bytes 400000 | tf_op jit(solution)/shard_map/own_density/pallas_call | solution.py:329
  43.9 0.0 collective-permute-done.1.upper_stat_ref.upper_ref
  43.9 0.0 copy-start.1
  43.9 0.0 collective-permute-done.lower_stat_ref.lower_ref
  43.9 0.0 copy-start.2
  43.9 4.2 %all-to-all-done = f32[128,8,128]{2,1,0:T(8,128)S(1)} async-done(((f32[128,8,128]{2,1,0:T(8,128)}), f32[128,8,128]{2,1,0:T(8,128)S(1)}, u32[]{:S(2)}, u32[]{:S(2)}) %all-to-all-start) | async-done | bytes 524320 | tf_op jit(solution)/shard_map/all_to_all | solution.py:632
  48.1 0.0 copy-start
  48.1 0.0 copy-done.1
  48.1 0.0 copy-done.2
  48.1 0.8 copy-done
  48.9 21.1 %feed.1 = (f32[64,128]{1,0:T(8,128)}, f32[128,8]{1,0:T(8,128)}, f32[24,128]{1,0:T(8,128)}, s32[24,128]{1,0:T(8,128)}) custom-call(s32[2,16]{1,0:T(2,128)} %bitcast.35, f32[6,64,128]{2,1,0:T(8,128)} %get-tuple-element.9.stat_ref.core_ref.sorted_ref, f32[6,64,128]{2,1,0:T(8,128)} %copy-done.2, f32[6,64,128]{2,1,0:T(8,128)} %copy-done.1, ...), custom_call_target="tpu_custom_call" | custom-call | flops 71303168 | bytes 2000000 | tf_op jit(solution)/shard_map/feed/pallas_call | solution.py:540
  70.1 9.2 %all-to-all-start.1 = ((f32[128,1,8]{2,1,0:T(1,128)}), f32[128,1,8]{2,1,0:T(1,128)S(1)}, u32[]{:S(2)}, u32[]{:S(2)}) async-start(f32[128,1,8]{2,1,0:T(1,128)} %bitcast.31), calls=%async_computation.1 | async-start | bytes 131072 | tf_op jit(solution)/shard_map/all_to_all | solution.py:652
  79.3 2.6 %apply.1 = f32[2,64,128]{2,1,0:T(8,128)} custom-call(f32[24,128]{1,0:T(8,128)} %get-tuple-element.12.lost_ref, s32[24,128]{1,0:T(8,128)} %get-tuple-element.13.gas_at_ref, f32[5,64,128]{2,1,0:T(8,128)} %bitcast.26, f32[64,128]{1,0:T(8,128)} %bitcast.29), custom_call_target="tpu_custom_call" | custom-call | flops 1000000 | bytes 100000 | tf_op jit(solution)/shard_map/apply/pallas_call | solution.py:587
  81.9 8.8 %all-to-all-done.1 = f32[128,1,8]{2,1,0:T(1,128)S(1)} async-done(((f32[128,1,8]{2,1,0:T(1,128)}), f32[128,1,8]{2,1,0:T(1,128)S(1)}, u32[]{:S(2)}, u32[]{:S(2)}) %all-to-all-start.1) | async-done | bytes 4128 | tf_op jit(solution)/shard_map/all_to_all | solution.py:652
  90.7 0.0 copy-start.3
  90.7 0.6 copy-done.3
  91.4 1.6 %settle.1 = f32[2,1,128]{2,1,0:T(1,128)} custom-call(f32[128,8]{1,0:T(8,128)} %bitcast.27), custom_call_target="tpu_custom_call" | custom-call | tf_op jit(solution)/shard_map/settle/pallas_call | solution.py:609
  (1 shorter events, 0.0 us)
Async XLA Ops:
  1.3 0.7 copy-start.4
  1.3 0.7 copy-start.5
  2.8 45.3 %all-to-all-start = ((f32[128,8,128]{2,1,0:T(8,128)}), f32[128,8,128]{2,1,0:T(8,128)S(1)}, u32[]{:S(2)}, u32[]{:S(2)}) async-start(f32[128,8,128]{2,1,0:T(8,128)} %broadcast_in_dim.2), calls=%async_computation | async-start | bytes 1048576 | tf_op jit(solution)/shard_map/all_to_all | solution.py:632
  30.7 13.2 %collective-permute-start.1 = (f32[6,64,128]{2,1,0:T(8,128)}, f32[6,64,128]{2,1,0:T(8,128)S(1)}, u32[]{:S(2)}, u32[]{:S(2)}) collective-permute-start(f32[6,64,128]{2,1,0:T(8,128)} %get-tuple-element.9.stat_ref.core_ref.sorted_ref), channel_id=1, source_target_pairs={{1,0},{2,1},{3,2},{4,3},{5,4},{6,5},{7,6},{8,7},{9,8},{10,9},{11,1... | collective-permute-start | bytes 589832 | tf_op jit(solution)/shard_map/ppermute | solution.py:627
  31.6 12.3 %collective-permute-start = (f32[6,64,128]{2,1,0:T(8,128)}, f32[6,64,128]{2,1,0:T(8,128)S(1)}, u32[]{:S(2)}, u32[]{:S(2)}) collective-permute-start(f32[6,64,128]{2,1,0:T(8,128)} %get-tuple-element.9.stat_ref.core_ref.sorted_ref), channel_id=1, source_target_pairs={{0,1},{1,2},{2,3},{3,4},{4,5},{5,6},{6,7},{7,8},{8,9},{9,10},{10,1... | collective-permute-start | bytes 589832 | tf_op jit(solution)/shard_map/ppermute | solution.py:626
  43.9 4.2 %copy-start.1 = (f32[6,64,128]{2,1,0:T(8,128)}, f32[6,64,128]{2,1,0:T(8,128)S(1)}, u32[]{:S(2)}) copy-start(f32[6,64,128]{2,1,0:T(8,128)S(1)} %collective-permute-done.1.upper_stat_ref.upper_ref) | copy-start | bytes 589828
  43.9 4.2 %copy-start.2 = (f32[6,64,128]{2,1,0:T(8,128)}, f32[6,64,128]{2,1,0:T(8,128)S(1)}, u32[]{:S(2)}) copy-start(f32[6,64,128]{2,1,0:T(8,128)S(1)} %collective-permute-done.lower_stat_ref.lower_ref) | copy-start | bytes 589828
  48.1 0.8 copy-start
  70.1 20.7 %all-to-all-start.1 = ((f32[128,1,8]{2,1,0:T(1,128)}), f32[128,1,8]{2,1,0:T(1,128)S(1)}, u32[]{:S(2)}, u32[]{:S(2)}) async-start(f32[128,1,8]{2,1,0:T(1,128)} %bitcast.31), calls=%async_computation.1 | async-start | bytes 131072 | tf_op jit(solution)/shard_map/all_to_all | solution.py:652
  90.7 0.6 copy-start.3

commit v3 on v2

--- a/solution.py
+++ b/solution.py
@@ -20,6 +20,8 @@
 TILES = LANES // 8
 BINS = 32768.0
 UNROLL = 16
+STATIC = 8
+GRANT = 16 * 1024 * 1024
 
 kernel_norm = 21.0 / (2.0 * math.pi)
 face_width = 32.0
@@ -161,13 +163,17 @@
 
 
 def run_corners(out_ref, cell, cols, rows, found):
-    for g, h, near in found:
-
-        @pl.when(near)
-        def _():
-            part = fold(corner_block(cols, rows[g], h)) * (4.0 * kernel_norm)
-            at = pl.ds(cell * GROUPS + g, 1)
-            out_ref[at, :] = out_ref[at, :] + part
+    some = functools.reduce(jnp.logical_or, [near for _, _, near in found])
+
+    @pl.when(some)
+    def _():
+        for g, h, near in found:
+
+            @pl.when(near)
+            def _():
+                part = fold(corner_block(cols, rows[g], h)) * (4.0 * kernel_norm)
+                at = pl.ds(cell * GROUPS + g, 1)
+                out_ref[at, :] = out_ref[at, :] + part
 
 
 def span(z):
@@ -294,6 +300,7 @@
         out_specs=(vmem(), vmem()),
         scratch_shapes=[pltpu.VMEM((ROWS, LANES), jnp.float32)],
         cost_estimate=pl.CostEstimate(flops=3000000, bytes_accessed=400000, transcendentals=0),
+compiler_params=pltpu.CompilerParams(vmem_limit_bytes=GRANT),
         name="order",
     )(core)
 
@@ -334,6 +341,7 @@
         scratch_shapes=[pltpu.VMEM((5, CELL, LANES), jnp.float32), pltpu.VMEM((CELL, LANES), jnp.float32)],
         cost_estimate=pl.CostEstimate(flops=CPD * CELL * CELL * 12, bytes_accessed=400000, transcendentals=0),
         grid=(1,),
+compiler_params=pltpu.CompilerParams(vmem_limit_bytes=GRANT),
         name="own_density",
     )(core, core)
 
@@ -354,10 +362,8 @@
     return rate, rate / limit, rho_hole
 
 
-def feed_kernel(
-    y_length,
+def pairs_kernel(
     z_length,
-    group,
     pairs_ref,
     stat_ref,
     lower_stat_ref,
@@ -372,16 +378,46 @@
     energy_ref,
     gas_id_ref,
     slot_ref,
-    count_ref,
-    holes_ref,
     rho_ref,
-    message_ref,
-    lost_ref,
-    gas_at_ref,
+    picked_ref,
+    place_ref,
     cells,
     cols,
     held_rho,
 ):
+    blocks = CAP // 8
+    lane = lax.broadcasted_iota(jnp.int32, (8, LANES), 1)
+    sub = lax.broadcasted_iota(jnp.int32, (8, LANES), 0)
+    coded = gas_id_ref[...] * LANES + slot_ref[...]
+    for v in range(blocks):
+        place = CAP * lane + (8 * v + sub)
+        place_row, place_lane = place >> 7, place & (LANES - 1)
+        piece = jnp.zeros((8, LANES), jnp.int32)
+        for r in range(CAP):
+            row = jnp.broadcast_to(coded[r : r + 1], (8, LANES))
+            piece = jnp.where(place_row == r, lane_take(row, place_lane), piece)
+        place_ref[8 * v : 8 * v + 8, :] = piece
+    sources = [(core_ref, 0), (core_ref, 1), (core_ref, 2)] + [(vel_ref, 0), (vel_ref, 1), (vel_ref, 2)]
+    sources = sources + [(core_ref, 3), (energy_ref, 0)]
+    per_step = ROWS // NPAIR
+
+    def pick(first, lines):
+        for v in range(blocks):
+            part = slice(8 * v, 8 * v + 8)
+            at = place_ref[part, :]
+            gas_row, gas_lane = at >> 14, (at >> 7) & (LANES - 1)
+            here = [gas_row == first + inner for inner in range(per_step)]
+            for field, (ref, plane) in lines:
+                value = picked_ref[field, part, :]
+                for inner in range(per_step):
+                    line = ref[pl.ds(first + inner, 1), :] if plane is None else ref[plane, pl.ds(first + inner, 1), :]
+                    moved = lane_take(jnp.broadcast_to(line, (8, LANES)), gas_lane)
+                    value = jnp.where(here[inner], moved, value)
+                picked_ref[field, part, :] = value
+
+    def pick_rows(step):
+        pick(step * per_step, list(enumerate(sources)))
+
     half = 0.5 * z_length
     low, high = span(sorted_ref[2])
     plain = high - low <= half
@@ -409,6 +445,7 @@
             other = pairs_ref[1, step]
             fill_cols(cols, load_cell(cells, other))
             rows = spread_rows(load_cell(sorted_ref, home))
+            pick_rows(step)
             put_total(held_rho, home, band_block(cols, rows), True)
 
             def corners(q_stat, q_cell):
@@ -427,6 +464,7 @@
         def _(step):
             home = pairs_ref[0, step]
             fill_cols(cols, load_cell(cells, pairs_ref[1, step]))
+            pick_rows(step)
             rows = spread_rows(load_cell(sorted_ref, home))
             put_total(held_rho, home, dense_block(cols, rows, z_length), True)
 
@@ -439,47 +477,39 @@
             value = jnp.where(group_at == other, moved, value)
         rho_ref[pl.ds(g, CPD, stride=GROUPS), :] = value
 
-    lane = lax.broadcasted_iota(jnp.int32, (8, LANES), 1)
-    sub = lax.broadcasted_iota(jnp.int32, (8, LANES), 0)
-    coded = gas_id_ref[...] * LANES + slot_ref[...]
-    turned = []
-    for v in range(CAP // 8):
-        place = CAP * lane + (8 * v + sub)
-        place_row, place_lane = place >> 7, place & (LANES - 1)
-        piece = jnp.zeros((8, LANES), jnp.int32)
-        for r in range(CAP):
-            row = jnp.broadcast_to(coded[r : r + 1], (8, LANES))
-            piece = jnp.where(place_row == r, lane_take(row, place_lane), piece)
-        turned.append(piece)
+    for step in range(NPAIR):
+        pick(step * per_step, [(STATIC, (rho_ref, None))])
+
+
+def pairs_density(pairs, ranked, lower, upper, own, back, core, vel, energy, gas_id, slot, z_length):
+    smem = pl.BlockSpec(memory_space=pltpu.SMEM)
+    return pl.pallas_call(
+        functools.partial(pairs_kernel, z_length),
+        out_shape=(
+            jax.ShapeDtypeStruct((ROWS, LANES), jnp.float32),
+            jax.ShapeDtypeStruct((STATIC + 1, CAP, LANES), jnp.float32),
+            jax.ShapeDtypeStruct((CAP, LANES), jnp.int32),
+        ),
+        in_specs=[smem] + [stat_spec()] * 3 + [vmem()] * 10,
+        out_specs=(vmem(),) * 3,
+        scratch_shapes=[
+            pltpu.VMEM((5, 2 * REACH + ROWS, LANES), jnp.float32),
+            pltpu.VMEM((5, CELL, LANES), jnp.float32),
+            pltpu.VMEM((ROWS, LANES), jnp.float32),
+        ],
+        cost_estimate=pl.CostEstimate(flops=NPAIR * CELL * CELL * 17, bytes_accessed=2000000, transcendentals=0),
+        grid=(1,),
+compiler_params=pltpu.CompilerParams(vmem_limit_bytes=GRANT),
+        name="pairs_density",
+    )(pairs, ranked, lower, upper, ranked, lower, upper, own, back, core, vel, energy, gas_id, slot)
+
+
+def feed_kernel(y_length, z_length, group, picked_ref, place_ref, count_ref, holes_ref, message_ref, lost_ref, gas_at_ref):
+    gas = [picked_ref[f] for f in range(STATIC + 1)]
+    place = place_ref[...]
+    slot = place & (LANES - 1)
     count = count_ref[...]
-    live = [(8 * v + sub) < count for v in range(CAP // 8)]
-    gas_row = [t >> 14 for t in turned]
-    gas_lane = [(t >> 7) & (LANES - 1) for t in turned]
-    slot = [t & (LANES - 1) for t in turned]
-
-    sources = [(core_ref, 0), (core_ref, 1), (core_ref, 2)] + [(vel_ref, 0), (vel_ref, 1), (vel_ref, 2)]
-    sources = sources + [(core_ref, 3), (energy_ref, None), (rho_ref, None)]
-    blocks = CAP // 8
-
-    def gather(turn, picked):
-        picked = list(picked)
-        for inner in range(4):
-            r = turn * 4 + inner
-            for f, (ref, plane) in enumerate(sources):
-                line = ref[pl.ds(r, 1), :] if plane is None else ref[plane, pl.ds(r, 1), :]
-                line = jnp.broadcast_to(line, (8, LANES))
-                for v in range(blocks):
-                    at = f * blocks + v
-                    picked[at] = jnp.where(gas_row[v] == r, lane_take(line, gas_lane[v]), picked[at])
-        return tuple(picked)
-
-    zero = jnp.zeros((8, LANES), jnp.float32)
-    picked = lax.fori_loop(0, ROWS // 4, gather, (zero,) * (9 * blocks))
-    gas = [jnp.concatenate(picked[f * blocks : (f + 1) * blocks], axis=0) for f in range(9)]
-    live = jnp.concatenate([l.astype(jnp.int32) for l in live], axis=0) > 0
-    slot = jnp.concatenate(slot, axis=0)
-    gas_row = jnp.concatenate(gas_row, axis=0)
-    gas_lane = jnp.concatenate(gas_lane, axis=0)
+    live = lax.broadcasted_iota(jnp.int32, (CAP, LANES), 0) < count
 
     first = slot[0:1]
     second = jnp.max(jnp.where(live & (slot != first), slot, -1), axis=0, keepdims=True)
@@ -532,30 +562,23 @@
     lines = jnp.concatenate(lines + [jnp.zeros((LANES - 8, LANES), jnp.float32)], axis=0)
     message_ref[...] = lines.T[:, 0:8]
     lost_ref[...] = lost
-    gas_at_ref[...] = gas_row * LANES + gas_lane
-
-
-def feed(pairs, ranked, lower, upper, own, back, core, vel, energy, gas_id, slot, count, holes, y_length, z_length, group):
-    smem = pl.BlockSpec(memory_space=pltpu.SMEM)
+    gas_at_ref[...] = place >> 7
+
+
+def feed(picked, place, count, holes, y_length, z_length, group):
     return pl.pallas_call(
         functools.partial(feed_kernel, y_length, z_length, group),
         out_shape=(
-            jax.ShapeDtypeStruct((ROWS, LANES), jnp.float32),
             jax.ShapeDtypeStruct((group, 8), jnp.float32),
             jax.ShapeDtypeStruct((CAP, LANES), jnp.float32),
             jax.ShapeDtypeStruct((CAP, LANES), jnp.int32),
         ),
-        in_specs=[smem] + [stat_spec()] * 3 + [vmem()] * 12,
-        out_specs=(vmem(),) * 4,
-        scratch_shapes=[
-            pltpu.VMEM((5, 2 * REACH + ROWS, LANES), jnp.float32),
-            pltpu.VMEM((5, CELL, LANES), jnp.float32),
-            pltpu.VMEM((ROWS, LANES), jnp.float32),
-        ],
-        cost_estimate=pl.CostEstimate(flops=NPAIR * CELL * CELL * 17, bytes_accessed=2000000, transcendentals=0),
-        grid=(1,),
+        in_specs=[vmem()] * 4,
+        out_specs=(vmem(),) * 3,
+        cost_estimate=pl.CostEstimate(flops=1000000, bytes_accessed=1000000, transcendentals=0),
+compiler_params=pltpu.CompilerParams(vmem_limit_bytes=GRANT),
         name="feed",
-    )(pairs, ranked, lower, upper, ranked, lower, upper, own, back, core, vel, energy, gas_id, slot, count, holes)
+    )(picked, place, count, holes)
 
 
 def apply_kernel(lost_ref, gas_at_ref, core_ref, energy_ref, update_ref):
@@ -591,8 +614,25 @@
         out_specs=vmem(),
         cost_estimate=pl.CostEstimate(flops=1000000, bytes_accessed=100000, transcendentals=0),
         grid=(1,),
+compiler_params=pltpu.CompilerParams(vmem_limit_bytes=GRANT),
         name="apply",
     )(lost, gas_at, core, energy)
+
+
+def spread_kernel(group, coord_ref, vel_ref, mass_ref, soft_ref, out_ref):
+    lines = [coord_ref[f] for f in range(3)] + [vel_ref[f] for f in range(3)] + [mass_ref[0], soft_ref[0]]
+    out_ref[...] = jnp.broadcast_to(jnp.concatenate(lines, axis=0)[None], (group, 8, LANES))
+
+
+def spread(coord, vel, mass, soft, group):
+    return pl.pallas_call(
+        functools.partial(spread_kernel, group),
+        out_shape=jax.ShapeDtypeStruct((group, 8, LANES), jnp.float32),
+        in_specs=[vmem()] * 4,
+        out_specs=vmem(),
+compiler_params=pltpu.CompilerParams(vmem_limit_bytes=GRANT),
+        name="spread",
+    )(coord, vel, mass, soft)
 
 
 def settle_kernel(group, arrived_ref, out_ref):
@@ -611,6 +651,7 @@
         out_shape=jax.ShapeDtypeStruct((2, 1, LANES), jnp.float32),
         in_specs=[vmem()],
         out_specs=vmem(),
+compiler_params=pltpu.CompilerParams(vmem_limit_bytes=GRANT),
         name="settle",
     )(arrived)
 
@@ -625,13 +666,16 @@
     ranked, back = order(core)
     lower = lax.ppermute(ranked, "dz", [(i, (i + 1) % deep) for i in range(deep)])
     upper = lax.ppermute(ranked, "dz", [((i + 1) % deep, i) for i in range(deep)])
-    table = jnp.concatenate(
-        [bh_coord.reshape(3, LANES), bh_vel.reshape(3, LANES), bh_mass.reshape(1, LANES), bh_soft.reshape(1, LANES)], 0
+    copies = spread(
+        bh_coord.reshape(3, 1, LANES),
+        bh_vel.reshape(3, 1, LANES),
+        bh_mass.reshape(1, 1, LANES),
+        bh_soft.reshape(1, 1, LANES),
+        group,
     )
-    copies = jnp.broadcast_to(table[None], (group, 8, LANES))
     holes = lax.all_to_all(copies, ("dy", "dz"), split_axis=0, concat_axis=0, tiled=True).reshape(group * 8, LANES)
     own = own_density(ranked, z_length)
-    rho, message, lost, gas_at = feed(
+    rho, picked, place = pairs_density(
         cell_pairs.reshape(2, NPAIR),
         ranked,
         lower,
@@ -640,15 +684,12 @@
         back,
         core,
         gas_vel.reshape(3, ROWS, LANES),
-        energy,
+        energy.reshape(1, ROWS, LANES),
         mem_gas.reshape(CAP, LANES),
         mem_slot.reshape(CAP, LANES),
-        send_count.reshape(1, LANES),
-        holes,
-        y_length,
         z_length,
-        group,
     )
+    message, lost, gas_at = feed(picked, place, send_count.reshape(1, LANES), holes, y_length, z_length, group)
     arrived = lax.all_to_all(message, ("dy", "dz"), split_axis=0, concat_axis=0, tiled=True)
     update = apply(lost, gas_at, core, energy)
     bh_update = settle(arrived, group)

time: 93.5 us -> 86.5 us (0.925)
  Pallas kernels: 40.2 us -> 32.9 us
  starting transfers between devices: 35.4 us -> 39.2 us
  waiting for transfers between devices: 13 us -> 10.8 us
  local copies, waits for them, and re-layouts: 3.61 us -> 2.65 us
    pallas_call x1, Pallas kernels: 21.1 us -> 1.27 us  [feed(): pl.pallas_call(functools.partial(feed_kernel, y_length, z_length, group),...]
    pallas_call x0 -> x2, Pallas kernels: none -> 16.8 us  [the longest x1 15.9 us: pairs_density(): pl.pallas_call(functools.partial(pairs_kernel, z_length), out_shape=(jax....]
    all_to_all x1, waiting for transfers between devices: 4.18 us -> 0.01 us  [body(): lax.all_to_all(copies, ('dy', 'dz'), split_axis=0, concat_axis=0, tiled=T...]
    all_to_all x1, starting transfers between devices: 9.21 us -> 12.9 us  [body(): lax.all_to_all(message, ('dy', 'dz'), split_axis=0, concat_axis=0, tiled=...]
    pallas_call x1, Pallas kernels: 3.44 us -> 1.84 us  [order(): pl.pallas_call(order_kernel, out_shape=(jax.ShapeDtypeStruct((6, ROWS, LA...]
    ppermute x1, waiting for transfers between devices: 0.01 us -> 1.14 us  [body(): lax.ppermute(ranked, 'dz', [((i + 1) % deep, i) for i in range(deep)])]
    pallas_call x1, Pallas kernels: 11.5 us -> 10.5 us  [own_density(): pl.pallas_call(functools.partial(own_kernel, z_length), out_shape=jax.Sha...]
    unnamed x13 -> x22, local copies, waits for them, and re-layouts: 2.78 us -> 2.65 us
  transfers between devices with their start and end apart: 4 -> 4, of which waited for: 2 -> 2; matrix products, arithmetic and copies ran while one was open for 0% -> 0% of each run, Pallas kernels for 19% -> 35%
where the time goes in v3:
time: 86.5 us; the launch traced here: 86.3 us
  starting transfers between devices  39.2 us (45%)
  Pallas kernels  32.9 us (38%)
  waiting for transfers between devices  10.8 us (12%)
  local copies, waits for them, and re-layouts  2.65 us (3%)
    all_to_all x1, starting transfers between devices, body(): lax.all_to_all(copies, ('dy', 'dz'), split_axis=0, concat_axis=0, tiled=T...  24.6 us
    pallas_call x1, Pallas kernels, pairs_density(): pl.pallas_call(functools.partial(pairs_kernel, z_length), out_shape=(jax....  15.9 us
    all_to_all x1, starting transfers between devices, body(): lax.all_to_all(message, ('dy', 'dz'), split_axis=0, concat_axis=0, tiled=...  12.9 us
    pallas_call x1, Pallas kernels, own_density(): pl.pallas_call(functools.partial(own_kernel, z_length), out_shape=jax.Sha...  10.5 us
    all_to_all x1, waiting for transfers between devices, body(): lax.all_to_all(message, ('dy', 'dz'), split_axis=0, concat_axis=0, tiled=...  9.66 us
    unnamed x22, local copies, waits for them, and re-layouts  2.65 us
    pallas_call x1, Pallas kernels, order(): pl.pallas_call(order_kernel, out_shape=(jax.ShapeDtypeStruct((6, ROWS, LA...  1.84 us
    pallas_call x1, Pallas kernels, apply(): pl.pallas_call(apply_kernel, out_shape=jax.ShapeDtypeStruct((2, ROWS, LAN...  1.8 us
  transfers between devices with their start and end apart: 4, of which 2 were waited for; matrix products, arithmetic and copies ran while one was open for 0% of the time, Pallas kernels for 35%

profile of v3, /device:TPU:1, one launch (start us, length us, event | category | flops | bytes accessed | tf_op | source)
XLA Modules:
  0.0 86.3 jit_solution(9431189387669818396)
XLA Ops:
  0.6 0.0 copy-start.6
  0.6 0.0 copy-start.5
  0.7 0.0 copy-start.8
  0.7 0.7 copy-done.6
  1.3 0.0 copy-done.5
  1.3 0.0 copy-done.8
  1.3 0.0 copy-start.9
  1.3 0.7 copy-done.9
  2.0 0.8 spread.1
  2.8 0.0 copy-start
  2.8 24.6 %all-to-all-start = ((f32[128,8,128]{2,1,0:T(8,128)}), f32[128,8,128]{2,1,0:T(8,128)S(1)}, u32[]{:S(2)}, u32[]{:S(2)}) async-start(f32[128,8,128]{2,1,0:T(8,128)} %spread.1), calls=%async_computation | async-start | bytes 1048576 | tf_op jit(solution)/shard_map/all_to_all | solution.py:676
  27.4 0.0 copy-done
  27.4 1.8 %order.1 = (f32[6,64,128]{2,1,0:T(8,128)S(1)}, s32[64,128]{1,0:T(8,128)S(1)}) custom-call(f32[5,64,128]{2,1,0:T(8,128)S(1)} %bitcast.21), custom_call_target="tpu_custom_call" | custom-call | flops 3000000 | bytes 400000 | tf_op jit(solution)/shard_map/order/pallas_call | solution.py:293
  29.3 0.0 copy-start.2
  29.3 0.9 %collective-permute-start.1 = (f32[6,64,128]{2,1,0:T(8,128)S(1)}, f32[6,64,128]{2,1,0:T(8,128)S(1)}, u32[]{:S(2)}, u32[]{:S(2)}) collective-permute-start(f32[6,64,128]{2,1,0:T(8,128)S(1)} %get-tuple-element.11.stat_ref.core_ref.sorted_ref), channel_id=1, source_target_pairs={{1,0},{2,1},{3,2},{4,3},{5,4},{6,5},{7,6},{8,7},{9,8},{10,9},{11,1... | collective-permute-start | bytes 589832 | tf_op jit(solution)/shard_map/ppermute | solution.py:668
  30.2 0.9 collective-permute-start
  31.0 0.0 copy-start.1
  31.0 0.0 copy-start.3
  31.0 0.0 copy-start.4
  31.0 10.5 %own_density.1.own_ref = f32[64,128]{1,0:T(8,128)S(1)} custom-call(f32[6,64,128]{2,1,0:T(8,128)S(1)} %get-tuple-element.11.stat_ref.core_ref.sorted_ref, f32[6,64,128]{2,1,0:T(8,128)S(1)} %get-tuple-element.11.stat_ref.core_ref.sorted_ref), custom_call_target="tpu_custom_call" | custom-call | flops 50331648 | bytes 400000 | tf_op jit(solution)/shard_map/own_density/pallas_call | solution.py:336
  41.5 1.1 %collective-permute-done.1.upper_stat_ref.upper_ref = f32[6,64,128]{2,1,0:T(8,128)S(1)} collective-permute-done((f32[6,64,128]{2,1,0:T(8,128)S(1)}, f32[6,64,128]{2,1,0:T(8,128)S(1)}, u32[]{:S(2)}, u32[]{:S(2)}) %collective-permute-start.1) | collective-permute-done | bytes 196640 | tf_op jit(solution)/shard_map/ppermute | solution.py:668
  42.7 0.0 collective-permute-done.lower_stat_ref.lower_ref
  42.7 0.0 copy-start.7
  42.7 0.0 copy-done.2
  42.7 0.0 copy-done.1
  42.7 0.0 copy-done.3
  42.7 0.0 copy-done.4
  42.7 0.6 copy-done.7
  43.4 15.9 %pairs_density.1 = (f32[64,128]{1,0:T(8,128)}, f32[9,24,128]{2,1,0:T(8,128)S(1)}, s32[24,128]{1,0:T(8,128)S(1)}) custom-call(s32[2,16]{1,0:T(2,128)S(1)} %bitcast.32, f32[6,64,128]{2,1,0:T(8,128)S(1)} %get-tuple-element.11.stat_ref.core_ref.sorted_ref, f32[6,64,128]{2,1,0:T(8,128)S(1)} %collective-permute-done.lower_stat_ref.lower_ref, ...), custom_call_target="tpu_custom_call" | custom-call | flops 71303168 | bytes 2000000 | tf_op jit(solution)/shard_map/pairs_density/pallas_call | solution.py:486
  59.3 0.0 all-to-all-done
  59.3 0.0 copy-start.10
  59.3 0.7 copy-done.10
  59.9 1.3 %feed.1 = (f32[128,8]{1,0:T(8,128)}, f32[24,128]{1,0:T(8,128)S(1)}, s32[24,128]{1,0:T(8,128)S(1)}) custom-call(f32[9,24,128]{2,1,0:T(8,128)S(1)} %get-tuple-element.14.picked_ref, s32[24,128]{1,0:T(8,128)S(1)} %get-tuple-element.15.place_ref, s32[1,128]{1,0:T(1,128)S(1)} %bitcast.33, f32[1024,128]{1,0:T(8,128)S(1)} %bitcast.20), custom_call_target="tpu_custom_call" | custom-call | flops 1000000 | bytes 1000000 | tf_op jit(solution)/shard_map/feed/pallas_call | solution.py:569
  61.2 12.9 %all-to-all-start.1 = ((f32[128,1,8]{2,1,0:T(1,128)}), f32[128,1,8]{2,1,0:T(1,128)S(1)}, u32[]{:S(2)}, u32[]{:S(2)}) async-start(f32[128,1,8]{2,1,0:T(1,128)} %bitcast.14), calls=%async_computation.1 | async-start | bytes 131072 | tf_op jit(solution)/shard_map/all_to_all | solution.py:693
  74.1 1.8 %apply.1 = f32[2,64,128]{2,1,0:T(8,128)} custom-call(f32[24,128]{1,0:T(8,128)S(1)} %get-tuple-element.16.lost_ref, s32[24,128]{1,0:T(8,128)S(1)} %get-tuple-element.17.gas_at_ref, f32[5,64,128]{2,1,0:T(8,128)S(1)} %bitcast.23, f32[64,128]{1,0:T(8,128)S(1)} %bitcast.26), custom_call_target="tpu_custom_call" | custom-call | flops 1000000 | bytes 100000 | tf_op jit(solution)/shard_map/apply/pallas_call | solution.py:610
  75.9 9.7 %all-to-all-done.1 = f32[128,1,8]{2,1,0:T(1,128)S(1)} async-done(((f32[128,1,8]{2,1,0:T(1,128)}), f32[128,1,8]{2,1,0:T(1,128)S(1)}, u32[]{:S(2)}, u32[]{:S(2)}) %all-to-all-start.1) | async-done | bytes 4128 | tf_op jit(solution)/shard_map/all_to_all | solution.py:693
  85.6 0.7 settle.1
Async XLA Ops:
  0.6 0.7 copy-start.6
  0.6 0.7 copy-start.5
  0.7 0.7 copy-start.8
  1.3 0.7 copy-start.9
  2.8 24.6 %copy-start = (f32[5,1,1,8192]{3,2,1,0:T(1,128)S(1)}, f32[5,1,1,8192]{3,2,1,0:T(1,128)}, u32[]{:S(2)}) copy-start(f32[5,1,1,8192]{3,2,1,0:T(1,128)} %param.11) | copy-start | bytes 491524
  2.8 56.4 %all-to-all-start = ((f32[128,8,128]{2,1,0:T(8,128)}), f32[128,8,128]{2,1,0:T(8,128)S(1)}, u32[]{:S(2)}, u32[]{:S(2)}) async-start(f32[128,8,128]{2,1,0:T(8,128)} %spread.1), calls=%async_computation | async-start | bytes 1048576 | tf_op jit(solution)/shard_map/all_to_all | solution.py:676
  29.3 13.4 %copy-start.2 = (f32[3,1,1,8192]{3,2,1,0:T(1,128)S(1)}, f32[3,1,1,8192]{3,2,1,0:T(1,128)}, u32[]{:S(2)}) copy-start(f32[3,1,1,8192]{3,2,1,0:T(1,128)} %param.12) | copy-start | bytes 294916
  29.3 13.4 %collective-permute-start.1 = (f32[6,64,128]{2,1,0:T(8,128)S(1)}, f32[6,64,128]{2,1,0:T(8,128)S(1)}, u32[]{:S(2)}, u32[]{:S(2)}) collective-permute-start(f32[6,64,128]{2,1,0:T(8,128)S(1)} %get-tuple-element.11.stat_ref.core_ref.sorted_ref), channel_id=1, source_target_pairs={{1,0},{2,1},{3,2},{4,3},{5,4},{6,5},{7,6},{8,7},{9,8},{10,9},{11,1... | collective-permute-start | bytes 589832 | tf_op jit(solution)/shard_map/ppermute | solution.py:668
  30.2 12.5 %collective-permute-start = (f32[6,64,128]{2,1,0:T(8,128)S(1)}, f32[6,64,128]{2,1,0:T(8,128)S(1)}, u32[]{:S(2)}, u32[]{:S(2)}) collective-permute-start(f32[6,64,128]{2,1,0:T(8,128)S(1)} %get-tuple-element.11.stat_ref.core_ref.sorted_ref), channel_id=1, source_target_pairs={{0,1},{1,2},{2,3},{3,4},{4,5},{5,6},{6,7},{7,8},{8,9},{9,10},{10,1... | collective-permute-start | bytes 589832 | tf_op jit(solution)/shard_map/ppermute | solution.py:667
  31.0 11.7 %copy-start.1 = (f32[1,1,8192]{2,1,0:T(1,128)S(1)}, f32[1,1,8192]{2,1,0:T(1,128)}, u32[]{:S(2)}) copy-start(f32[1,1,8192]{2,1,0:T(1,128)} %param.13) | copy-start | bytes 98308
  31.0 11.7 %copy-start.3 = (s32[1,1,3072]{2,1,0:T(1,128)S(1)}, s32[1,1,3072]{2,1,0:T(1,128)}, u32[]{:S(2)}) copy-start(s32[1,1,3072]{2,1,0:T(1,128)} %param.19) | copy-start | bytes 36868
  31.0 11.7 %copy-start.4 = (s32[1,1,3072]{2,1,0:T(1,128)S(1)}, s32[1,1,3072]{2,1,0:T(1,128)}, u32[]{:S(2)}) copy-start(s32[1,1,3072]{2,1,0:T(1,128)} %param.20) | copy-start | bytes 36868
  42.7 0.7 copy-start.7
  59.3 0.7 copy-start.10
  61.2 24.4 %all-to-all-start.1 = ((f32[128,1,8]{2,1,0:T(1,128)}), f32[128,1,8]{2,1,0:T(1,128)S(1)}, u32[]{:S(2)}, u32[]{:S(2)}) async-start(f32[128,1,8]{2,1,0:T(1,128)} %bitcast.14), calls=%async_computation.1 | async-start | bytes 131072 | tf_op jit(solution)/shard_map/all_to_all | solution.py:693

commit v4 on v3

--- a/solution.py
+++ b/solution.py
@@ -247,7 +247,7 @@
     return key - jnp.floor(key * (1.0 / CELL)) * CELL
 
 
-def order_kernel(core_ref, out_ref, back_ref, spare):
+def order_kernel(core_ref, out_ref, back_ref, tail_ref, head_ref, spare):
     lane = lax.broadcasted_iota(jnp.int32, (CPD, LANES), 1)
     x = [by_group(core_ref, 0, g) for g in range(GROUPS)]
     low = jnp.min(jnp.minimum(jnp.minimum(x[0], x[1]), jnp.minimum(x[2], x[3])), axis=1, keepdims=True)
@@ -287,6 +287,8 @@
     for g in range(GROUPS):
         stat = jnp.where(lane == 0, lows[g], jnp.where(lane == 1, highs[g], tops))
         out_ref[5, pl.ds(g, CPD, stride=GROUPS), :] = stat
+    tail_ref[...] = out_ref[:, ROWS - REACH : ROWS, :]
+    head_ref[...] = out_ref[:, 0:REACH, :]
 
 
 def order(core):
@@ -295,9 +297,11 @@
         out_shape=(
             jax.ShapeDtypeStruct((6, ROWS, LANES), jnp.float32),
             jax.ShapeDtypeStruct((ROWS, LANES), jnp.int32),
+            jax.ShapeDtypeStruct((6, REACH, LANES), jnp.float32),
+            jax.ShapeDtypeStruct((6, REACH, LANES), jnp.float32),
         ),
         in_specs=[vmem()],
-        out_specs=(vmem(), vmem()),
+        out_specs=(vmem(),) * 4,
         scratch_shapes=[pltpu.VMEM((ROWS, LANES), jnp.float32)],
         cost_estimate=pl.CostEstimate(flops=3000000, bytes_accessed=400000, transcendentals=0),
 compiler_params=pltpu.CompilerParams(vmem_limit_bytes=GRANT),
@@ -328,8 +332,8 @@
             put_total(out_ref, cell, dense_block(cols, spread_rows(fields), z_length), False)
 
 
-def stat_spec():
-    return pl.BlockSpec((1, ROWS, LANES), lambda i: (5, 0, 0), memory_space=pltpu.SMEM)
+def stat_spec(rows=ROWS):
+    return pl.BlockSpec((1, rows, LANES), lambda i: (5, 0, 0), memory_space=pltpu.SMEM)
 
 
 def own_density(core, z_length):
@@ -421,7 +425,7 @@
     half = 0.5 * z_length
     low, high = span(sorted_ref[2])
     plain = high - low <= half
-    edges = ((lower_ref, slice(ROWS - REACH, ROWS), 0), (upper_ref, slice(0, REACH), REACH + ROWS))
+    edges = ((lower_ref, slice(0, REACH), 0), (upper_ref, slice(0, REACH), REACH + ROWS))
     for ref, part, at in edges:
         z = ref[2, part, :]
         edge_low, edge_high = span(z)
@@ -451,7 +455,7 @@
             def corners(q_stat, q_cell):
                 run_corners(held_rho, home, cols, rows, far_groups(stat_ref, home, q_stat, q_cell))
 
-            pl.when(other < BND)(lambda: corners(lower_stat_ref, other + (CPD - BND)))
+            pl.when(other < BND)(lambda: corners(lower_stat_ref, other))
             pl.when(other >= BND + CPD)(lambda: corners(upper_stat_ref, other - (BND + CPD)))
             pl.when(jnp.logical_and(other >= BND, other < BND + CPD))(lambda: corners(stat_ref, other - BND))
 
@@ -490,7 +494,7 @@
             jax.ShapeDtypeStruct((STATIC + 1, CAP, LANES), jnp.float32),
             jax.ShapeDtypeStruct((CAP, LANES), jnp.int32),
         ),
-        in_specs=[smem] + [stat_spec()] * 3 + [vmem()] * 10,
+        in_specs=[smem, stat_spec(), stat_spec(REACH), stat_spec(REACH)] + [vmem()] * 10,
         out_specs=(vmem(),) * 3,
         scratch_shapes=[
             pltpu.VMEM((5, 2 * REACH + ROWS, LANES), jnp.float32),
@@ -619,20 +623,26 @@
     )(lost, gas_at, core, energy)
 
 
-def spread_kernel(group, coord_ref, vel_ref, mass_ref, soft_ref, out_ref):
+def spread_kernel(group, coord_ref, vel_ref, mass_ref, soft_ref, pairs_ref, count_ref, out_ref, pairs_out, count_out):
+    pairs_out[...] = pairs_ref[...]
+    count_out[...] = count_ref[...]
     lines = [coord_ref[f] for f in range(3)] + [vel_ref[f] for f in range(3)] + [mass_ref[0], soft_ref[0]]
     out_ref[...] = jnp.broadcast_to(jnp.concatenate(lines, axis=0)[None], (group, 8, LANES))
 
 
-def spread(coord, vel, mass, soft, group):
+def spread(coord, vel, mass, soft, pairs, count, group):
     return pl.pallas_call(
         functools.partial(spread_kernel, group),
-        out_shape=jax.ShapeDtypeStruct((group, 8, LANES), jnp.float32),
-        in_specs=[vmem()] * 4,
-        out_specs=vmem(),
-compiler_params=pltpu.CompilerParams(vmem_limit_bytes=GRANT),
+        out_shape=(
+            jax.ShapeDtypeStruct((group, 8, LANES), jnp.float32),
+            jax.ShapeDtypeStruct((2, NPAIR), jnp.int32),
+            jax.ShapeDtypeStruct((1, LANES), jnp.int32),
+        ),
+        in_specs=[vmem()] * 6,
+        out_specs=(vmem(),) * 3,
+        compiler_params=pltpu.CompilerParams(vmem_limit_bytes=GRANT),
         name="spread",
-    )(coord, vel, mass, soft)
+    )(coord, vel, mass, soft, pairs, count)
 
 
 def settle_kernel(group, arrived_ref, out_ref):
@@ -663,20 +673,22 @@
     y_length = face_width * lax.axis_size("dy")
     core = gas_core.reshape(5, ROWS, LANES)
     energy = gas_energy.reshape(ROWS, LANES)
-    ranked, back = order(core)
-    lower = lax.ppermute(ranked, "dz", [(i, (i + 1) % deep) for i in range(deep)])
-    upper = lax.ppermute(ranked, "dz", [((i + 1) % deep, i) for i in range(deep)])
-    copies = spread(
+    ranked, back, tail, head = order(core)
+    lower = lax.ppermute(tail, "dz", [(i, (i + 1) % deep) for i in range(deep)])
+    upper = lax.ppermute(head, "dz", [((i + 1) % deep, i) for i in range(deep)])
+    copies, pairs, count = spread(
         bh_coord.reshape(3, 1, LANES),
         bh_vel.reshape(3, 1, LANES),
         bh_mass.reshape(1, 1, LANES),
         bh_soft.reshape(1, 1, LANES),
+        cell_pairs.reshape(2, NPAIR),
+        send_count.reshape(1, LANES),
         group,
     )
     holes = lax.all_to_all(copies, ("dy", "dz"), split_axis=0, concat_axis=0, tiled=True).reshape(group * 8, LANES)
     own = own_density(ranked, z_length)
     rho, picked, place = pairs_density(
-        cell_pairs.reshape(2, NPAIR),
+        pairs,
         ranked,
         lower,
         upper,
@@ -689,7 +701,7 @@
         mem_slot.reshape(CAP, LANES),
         z_length,
     )
-    message, lost, gas_at = feed(picked, place, send_count.reshape(1, LANES), holes, y_length, z_length, group)
+    message, lost, gas_at = feed(picked, place, count, holes, y_length, z_length, group)
     arrived = lax.all_to_all(message, ("dy", "dz"), split_axis=0, concat_axis=0, tiled=True)
     update = apply(lost, gas_at, core, energy)
     bh_update = settle(arrived, group)

time: 86.5 us -> 85 us (0.983)
  local copies, waits for them, and re-layouts: 2.65 us -> 0.72 us
  starting transfers between devices: 39.2 us -> 40.9 us
    unnamed x22, local copies, waits for them, and re-layouts: 2.65 us -> 0.72 us
    all_to_all x1, starting transfers between devices: 12.9 us -> 14.7 us  [body(): lax.all_to_all(message, ('dy', 'dz'), split_axis=0, concat_axis=0, tiled=...]
where the time goes in v4:
time: 85 us; the launch traced here: 84.7 us
  starting transfers between devices  40.9 us (48%)
  Pallas kernels  32.3 us (38%)
  waiting for transfers between devices  10.1 us (12%)
    all_to_all x1, starting transfers between devices, body(): lax.all_to_all(copies, ('dy', 'dz'), split_axis=0, concat_axis=0, tiled=T...  24.6 us
    pallas_call x1, Pallas kernels, pairs_density(): pl.pallas_call(functools.partial(pairs_kernel, z_length), out_shape=(jax....  15.3 us
    all_to_all x1, starting transfers between devices, body(): lax.all_to_all(message, ('dy', 'dz'), split_axis=0, concat_axis=0, tiled=...  14.7 us
    pallas_call x1, Pallas kernels, own_density(): pl.pallas_call(functools.partial(own_kernel, z_length), out_shape=jax.Sha...  10.5 us
    all_to_all x1, waiting for transfers between devices, body(): lax.all_to_all(message, ('dy', 'dz'), split_axis=0, concat_axis=0, tiled=...  9.68 us
    pallas_call x1, Pallas kernels, order(): pl.pallas_call(order_kernel, out_shape=(jax.ShapeDtypeStruct((6, ROWS, LA...  1.86 us
    pallas_call x1, Pallas kernels, apply(): pl.pallas_call(apply_kernel, out_shape=jax.ShapeDtypeStruct((2, ROWS, LAN...  1.81 us
  transfers between devices with their start and end apart: 4, of which 2 were waited for; matrix products, arithmetic and copies ran while one was open for 0% of the time, Pallas kernels for 35%

profile of v4, /device:TPU:1, one launch (start us, length us, event | category | flops | bytes accessed | tf_op | source)
XLA Modules:
  0.0 84.7 jit_solution(18341936948938685746)
XLA Ops:
  0.6 0.0 copy-start.7
  0.6 0.0 copy-start.9
  0.7 0.0 copy-start.10
  0.7 0.0 copy-start.5
  0.7 0.0 copy-start.6
  0.7 0.0 copy-start.8
  0.7 0.6 copy-done.7
  1.3 0.0 copy-done.9
  1.3 0.0 copy-done.10
  1.3 0.0 copy-done.5
  1.4 0.0 copy-done.6
  1.4 0.0 copy-done.8
  1.4 0.8 spread.1
  2.2 0.0 copy-start
  2.2 24.6 %all-to-all-start = ((f32[128,8,128]{2,1,0:T(8,128)}), f32[128,8,128]{2,1,0:T(8,128)S(1)}, u32[]{:S(2)}, u32[]{:S(2)}) async-start(f32[128,8,128]{2,1,0:T(8,128)} %get-tuple-element.25), calls=%async_computation | async-start | bytes 1048576 | tf_op jit(solution)/shard_map/all_to_all | solution.py:688
  26.8 0.0 copy-done
  26.8 1.9 %order.1 = (f32[6,64,128]{2,1,0:T(8,128)S(1)}, s32[64,128]{1,0:T(8,128)S(1)}, f32[6,40,128]{2,1,0:T(8,128)S(1)}, f32[6,40,128]{2,1,0:T(8,128)S(1)}) custom-call(f32[5,64,128]{2,1,0:T(8,128)S(1)} %bitcast.21), custom_call_target="tpu_custom_call" | custom-call | flops 3000000 | bytes 400000 | tf_op jit(solution)/shard_map/order/pallas_call | solution.py:295
  28.7 1.6 %collective-permute-start = (f32[6,40,128]{2,1,0:T(8,128)S(1)}, f32[6,40,128]{2,1,0:T(8,128)S(1)}, u32[]{:S(2)}, u32[]{:S(2)}) collective-permute-start(f32[6,40,128]{2,1,0:T(8,128)S(1)} %get-tuple-element.18), channel_id=1, source_target_pairs={{0,1},{1,2},{2,3},{3,4},{4,5},{5,6},{6,7},{7,8},{8,9},{9,10},{10,1... | collective-permute-start | bytes 368648 | tf_op jit(solution)/shard_map/ppermute | solution.py:677
  30.3 0.0 collective-permute-start.1
  30.3 0.0 copy-start.1
  30.3 0.0 copy-start.2
  30.3 0.0 copy-start.3
  30.3 0.0 copy-start.4
  30.3 10.5 %own_density.1.own_ref = f32[64,128]{1,0:T(8,128)S(1)} custom-call(f32[6,64,128]{2,1,0:T(8,128)S(1)} %get-tuple-element.17.stat_ref.core_ref.sorted_ref, f32[6,64,128]{2,1,0:T(8,128)S(1)} %get-tuple-element.17.stat_ref.core_ref.sorted_ref), custom_call_target="tpu_custom_call" | custom-call | flops 50331648 | bytes 400000 | tf_op jit(solution)/shard_map/own_density/pallas_call | solution.py:340
  40.8 0.0 collective-permute-done.lower_stat_ref.lower_ref
  40.9 0.4 collective-permute-done.1.upper_stat_ref.upper_ref
  41.3 0.0 copy-done.1
  41.3 0.0 copy-done.2
  41.3 0.0 copy-done.3
  41.3 0.0 copy-done.4
  41.3 15.3 %pairs_density.1 = (f32[64,128]{1,0:T(8,128)}, f32[9,24,128]{2,1,0:T(8,128)S(1)}, s32[24,128]{1,0:T(8,128)S(1)}) custom-call(s32[2,16]{1,0:T(2,128)S(1)} %get-tuple-element.16.pairs_ref, f32[6,64,128]{2,1,0:T(8,128)S(1)} %get-tuple-element.17.stat_ref.core_ref.sorted_ref, f32[6,40,128]{2,1,0:T(8,128)S(1)} %collective-permute-done.lower_stat_ref.lower_ref, ...), custom_call_target="tpu_custom_call" | custom-call | flops 71303168 | bytes 2000000 | tf_op jit(solution)/shard_map/pairs_density/pallas_call | solution.py:490
  56.6 0.0 all-to-all-done
  56.6 1.3 %feed.1 = (f32[128,8]{1,0:T(8,128)}, f32[24,128]{1,0:T(8,128)S(1)}, s32[24,128]{1,0:T(8,128)S(1)}) custom-call(f32[9,24,128]{2,1,0:T(8,128)S(1)} %get-tuple-element.22.picked_ref, s32[24,128]{1,0:T(8,128)S(1)} %get-tuple-element.23.place_ref, s32[1,128]{1,0:T(1,128)S(1)} %get-tuple-element.24.count_ref, f32[1024,128]{1,0:T(8,128)S(1)} %bitcast.20), custom_call_target="tpu_custom_call" | custom-call | flops 1000000 | bytes 1000000 | tf_op jit(solution)/shard_map/feed/pallas_call | solution.py:573
  57.8 14.7 %all-to-all-start.1 = ((f32[128,1,8]{2,1,0:T(1,128)}), f32[128,1,8]{2,1,0:T(1,128)S(1)}, u32[]{:S(2)}, u32[]{:S(2)}) async-start(f32[128,1,8]{2,1,0:T(1,128)} %bitcast.14), calls=%async_computation.1 | async-start | bytes 131072 | tf_op jit(solution)/shard_map/all_to_all | solution.py:705
  72.5 1.8 %apply.1 = f32[2,64,128]{2,1,0:T(8,128)} custom-call(f32[24,128]{1,0:T(8,128)S(1)} %get-tuple-element.26.lost_ref, s32[24,128]{1,0:T(8,128)S(1)} %get-tuple-element.27.gas_at_ref, f32[5,64,128]{2,1,0:T(8,128)S(1)} %bitcast.23, f32[64,128]{1,0:T(8,128)S(1)} %bitcast.26), custom_call_target="tpu_custom_call" | custom-call | flops 1000000 | bytes 100000 | tf_op jit(solution)/shard_map/apply/pallas_call | solution.py:614
  74.3 9.7 %all-to-all-done.1 = f32[128,1,8]{2,1,0:T(1,128)S(1)} async-done(((f32[128,1,8]{2,1,0:T(1,128)}), f32[128,1,8]{2,1,0:T(1,128)S(1)}, u32[]{:S(2)}, u32[]{:S(2)}) %all-to-all-start.1) | async-done | bytes 4128 | tf_op jit(solution)/shard_map/all_to_all | solution.py:705
  84.0 0.7 settle.1
Async XLA Ops:
  0.6 0.7 copy-start.7
  0.6 0.7 copy-start.9
  0.7 0.7 copy-start.10
  0.7 0.7 copy-start.5
  0.7 0.7 copy-start.6
  0.7 0.7 copy-start.8
  2.2 24.6 %copy-start = (f32[5,1,1,8192]{3,2,1,0:T(1,128)S(1)}, f32[5,1,1,8192]{3,2,1,0:T(1,128)}, u32[]{:S(2)}) copy-start(f32[5,1,1,8192]{3,2,1,0:T(1,128)} %param.11) | copy-start | bytes 491524
  2.2 54.3 %all-to-all-start = ((f32[128,8,128]{2,1,0:T(8,128)}), f32[128,8,128]{2,1,0:T(8,128)S(1)}, u32[]{:S(2)}, u32[]{:S(2)}) async-start(f32[128,8,128]{2,1,0:T(8,128)} %get-tuple-element.25), calls=%async_computation | async-start | bytes 1048576 | tf_op jit(solution)/shard_map/all_to_all | solution.py:688
  28.7 12.2 %collective-permute-start = (f32[6,40,128]{2,1,0:T(8,128)S(1)}, f32[6,40,128]{2,1,0:T(8,128)S(1)}, u32[]{:S(2)}, u32[]{:S(2)}) collective-permute-start(f32[6,40,128]{2,1,0:T(8,128)S(1)} %get-tuple-element.18), channel_id=1, source_target_pairs={{0,1},{1,2},{2,3},{3,4},{4,5},{5,6},{6,7},{7,8},{8,9},{9,10},{10,1... | collective-permute-start | bytes 368648 | tf_op jit(solution)/shard_map/ppermute | solution.py:677
  30.3 11.0 %collective-permute-start.1 = (f32[6,40,128]{2,1,0:T(8,128)S(1)}, f32[6,40,128]{2,1,0:T(8,128)S(1)}, u32[]{:S(2)}, u32[]{:S(2)}) collective-permute-start(f32[6,40,128]{2,1,0:T(8,128)S(1)} %get-tuple-element.19), channel_id=1, source_target_pairs={{1,0},{2,1},{3,2},{4,3},{5,4},{6,5},{7,6},{8,7},{9,8},{10,9},{11,1... | collective-permute-start | bytes 368648 | tf_op jit(solution)/shard_map/ppermute | solution.py:678
  30.3 11.0 %copy-start.1 = (f32[1,1,8192]{2,1,0:T(1,128)S(1)}, f32[1,1,8192]{2,1,0:T(1,128)}, u32[]{:S(2)}) copy-start(f32[1,1,8192]{2,1,0:T(1,128)} %param.13) | copy-start | bytes 98308
  30.3 11.0 %copy-start.2 = (f32[3,1,1,8192]{3,2,1,0:T(1,128)S(1)}, f32[3,1,1,8192]{3,2,1,0:T(1,128)}, u32[]{:S(2)}) copy-start(f32[3,1,1,8192]{3,2,1,0:T(1,128)} %param.12) | copy-start | bytes 294916
  30.3 11.0 %copy-start.3 = (s32[1,1,3072]{2,1,0:T(1,128)S(1)}, s32[1,1,3072]{2,1,0:T(1,128)}, u32[]{:S(2)}) copy-start(s32[1,1,3072]{2,1,0:T(1,128)} %param.19) | copy-start | bytes 36868
  30.3 11.0 %copy-start.4 = (s32[1,1,3072]{2,1,0:T(1,128)S(1)}, s32[1,1,3072]{2,1,0:T(1,128)}, u32[]{:S(2)}) copy-start(s32[1,1,3072]{2,1,0:T(1,128)} %param.20) | copy-start | bytes 36868
  57.8 26.2 %all-to-all-start.1 = ((f32[128,1,8]{2,1,0:T(1,128)}), f32[128,1,8]{2,1,0:T(1,128)S(1)}, u32[]{:S(2)}, u32[]{:S(2)}) async-start(f32[128,1,8]{2,1,0:T(1,128)} %bitcast.14), calls=%async_computation.1 | async-start | bytes 131072 | tf_op jit(solution)/shard_map/all_to_all | solution.py:705

commit v5 on v4

--- a/solution.py
+++ b/solution.py
@@ -149,14 +149,14 @@
 
 
 def far_groups(p_stat, p_cell, q_stat, q_cell):
-    reach = p_stat[0, p_cell * GROUPS, 2] + q_stat[0, q_cell * GROUPS, 2]
+    reach = p_stat[0, 2, p_cell * GROUPS] + q_stat[0, 2, q_cell * GROUPS]
     reach = reach * 1.0001
     found = []
     for g in range(GROUPS):
         for h in range(GROUPS):
             if abs(g - h) >= 2:
-                p_low, p_high = p_stat[0, p_cell * GROUPS + g, 0], p_stat[0, p_cell * GROUPS + g, 1]
-                q_low, q_high = q_stat[0, q_cell * GROUPS + h, 0], q_stat[0, q_cell * GROUPS + h, 1]
+                p_low, p_high = p_stat[0, 0, p_cell * GROUPS + g], p_stat[0, 1, p_cell * GROUPS + g]
+                q_low, q_high = q_stat[0, 0, q_cell * GROUPS + h], q_stat[0, 1, q_cell * GROUPS + h]
                 near = jnp.logical_and(p_low - q_high <= reach, q_low - p_high <= reach)
                 found.append((g, h, near))
     return found
@@ -289,6 +289,10 @@
         out_ref[5, pl.ds(g, CPD, stride=GROUPS), :] = stat
     tail_ref[...] = out_ref[:, ROWS - REACH : ROWS, :]
     head_ref[...] = out_ref[:, 0:REACH, :]
+    turned = out_ref[5].T[0:8]
+    turned = jnp.concatenate([turned, turned], axis=1)
+    for ref in (out_ref, tail_ref, head_ref):
+        ref[5, 0:8, :] = turned
 
 
 def order(core):
@@ -332,8 +336,8 @@
             put_total(out_ref, cell, dense_block(cols, spread_rows(fields), z_length), False)
 
 
-def stat_spec(rows=ROWS):
-    return pl.BlockSpec((1, rows, LANES), lambda i: (5, 0, 0), memory_space=pltpu.SMEM)
+def stat_spec():
+    return pl.BlockSpec((1, 8, LANES), lambda i: (5, 0, 0), memory_space=pltpu.SMEM)
 
 
 def own_density(core, z_length):
@@ -455,7 +459,7 @@
             def corners(q_stat, q_cell):
                 run_corners(held_rho, home, cols, rows, far_groups(stat_ref, home, q_stat, q_cell))
 
-            pl.when(other < BND)(lambda: corners(lower_stat_ref, other))
+            pl.when(other < BND)(lambda: corners(lower_stat_ref, other + (CPD - BND)))
             pl.when(other >= BND + CPD)(lambda: corners(upper_stat_ref, other - (BND + CPD)))
             pl.when(jnp.logical_and(other >= BND, other < BND + CPD))(lambda: corners(stat_ref, other - BND))
 
@@ -494,7 +498,7 @@
             jax.ShapeDtypeStruct((STATIC + 1, CAP, LANES), jnp.float32),
             jax.ShapeDtypeStruct((CAP, LANES), jnp.int32),
         ),
-        in_specs=[smem, stat_spec(), stat_spec(REACH), stat_spec(REACH)] + [vmem()] * 10,
+        in_specs=[smem] + [stat_spec()] * 3 + [vmem()] * 10,
         out_specs=(vmem(),) * 3,
         scratch_shapes=[
             pltpu.VMEM((5, 2 * REACH + ROWS, LANES), jnp.float32),

time: 85 us -> 83.8 us (0.986)
  Pallas kernels: 32.3 us -> 31.1 us
  transfers between devices with their start and end apart: 4 -> 4, of which waited for: 2 -> 2; matrix products, arithmetic and copies ran while one was open for 0% -> 0% of each run, Pallas kernels for 35% -> 34%
where the time goes in v5:
time: 83.8 us; the launch traced here: 83.6 us
  starting transfers between devices  40.4 us (48%)
  Pallas kernels  31.1 us (37%)
  waiting for transfers between devices  10.6 us (13%)
    all_to_all x1, starting transfers between devices, body(): lax.all_to_all(copies, ('dy', 'dz'), split_axis=0, concat_axis=0, tiled=T...  24.6 us
    pallas_call x1, Pallas kernels, pairs_density(): pl.pallas_call(functools.partial(pairs_kernel, z_length), out_shape=(jax....  14.6 us
    all_to_all x1, starting transfers between devices, body(): lax.all_to_all(message, ('dy', 'dz'), split_axis=0, concat_axis=0, tiled=...  14.2 us
    pallas_call x1, Pallas kernels, own_density(): pl.pallas_call(functools.partial(own_kernel, z_length), out_shape=jax.Sha...  10 us
    all_to_all x1, waiting for transfers between devices, body(): lax.all_to_all(message, ('dy', 'dz'), split_axis=0, concat_axis=0, tiled=...  9.68 us
    pallas_call x1, Pallas kernels, apply(): pl.pallas_call(apply_kernel, out_shape=jax.ShapeDtypeStruct((2, ROWS, LAN...  1.81 us
    pallas_call x1, Pallas kernels, order(): pl.pallas_call(order_kernel, out_shape=(jax.ShapeDtypeStruct((6, ROWS, LA...  1.8 us
  transfers between devices with their start and end apart: 4, of which 2 were waited for; matrix products, arithmetic and copies ran while one was open for 0% of the time, Pallas kernels for 34%

profile of v5, /device:TPU:1, one launch (start us, length us, event | category | flops | bytes accessed | tf_op | source)
XLA Modules:
  0.0 83.6 jit_solution(9366387785018539232)
XLA Ops:
  0.6 0.0 copy-start.7
  0.6 0.0 copy-start.9
  0.7 0.0 copy-start.10
  0.7 0.0 copy-start.5
  0.7 0.0 copy-start.6
  0.7 0.0 copy-start.8
  0.7 0.6 copy-done.7
  1.3 0.0 copy-done.9
  1.3 0.0 copy-done.10
  1.3 0.0 copy-done.5
  1.4 0.0 copy-done.6
  1.4 0.0 copy-done.8
  1.4 0.8 spread.1
  2.2 0.0 copy-start
  2.2 24.6 %all-to-all-start = ((f32[128,8,128]{2,1,0:T(8,128)}), f32[128,8,128]{2,1,0:T(8,128)S(1)}, u32[]{:S(2)}, u32[]{:S(2)}) async-start(f32[128,8,128]{2,1,0:T(8,128)} %get-tuple-element.25), calls=%async_computation | async-start | bytes 1048576 | tf_op jit(solution)/shard_map/all_to_all | solution.py:692
  26.8 0.0 copy-done
  26.8 1.8 %order.1 = (f32[6,64,128]{2,1,0:T(8,128)S(1)}, s32[64,128]{1,0:T(8,128)S(1)}, f32[6,40,128]{2,1,0:T(8,128)S(1)}, f32[6,40,128]{2,1,0:T(8,128)S(1)}) custom-call(f32[5,64,128]{2,1,0:T(8,128)S(1)} %bitcast.21), custom_call_target="tpu_custom_call" | custom-call | flops 3000000 | bytes 400000 | tf_op jit(solution)/shard_map/order/pallas_call | solution.py:299
  28.6 1.6 %collective-permute-start = (f32[6,40,128]{2,1,0:T(8,128)S(1)}, f32[6,40,128]{2,1,0:T(8,128)S(1)}, u32[]{:S(2)}, u32[]{:S(2)}) collective-permute-start(f32[6,40,128]{2,1,0:T(8,128)S(1)} %get-tuple-element.18), channel_id=1, source_target_pairs={{0,1},{1,2},{2,3},{3,4},{4,5},{5,6},{6,7},{7,8},{8,9},{9,10},{10,1... | collective-permute-start | bytes 368648 | tf_op jit(solution)/shard_map/ppermute | solution.py:681
  30.2 0.0 collective-permute-start.1
  30.2 0.0 copy-start.1
  30.2 0.0 copy-start.2
  30.2 0.0 copy-start.3
  30.3 0.0 copy-start.4
  30.3 10.0 %own_density.1.own_ref = f32[64,128]{1,0:T(8,128)S(1)} custom-call(f32[6,64,128]{2,1,0:T(8,128)S(1)} %get-tuple-element.17.stat_ref.core_ref.sorted_ref, f32[6,64,128]{2,1,0:T(8,128)S(1)} %get-tuple-element.17.stat_ref.core_ref.sorted_ref), custom_call_target="tpu_custom_call" | custom-call | flops 50331648 | bytes 400000 | tf_op jit(solution)/shard_map/own_density/pallas_call | solution.py:344
  40.3 0.0 collective-permute-done.lower_stat_ref.lower_ref
  40.3 0.9 %collective-permute-done.1.upper_stat_ref.upper_ref = f32[6,40,128]{2,1,0:T(8,128)S(1)} collective-permute-done((f32[6,40,128]{2,1,0:T(8,128)S(1)}, f32[6,40,128]{2,1,0:T(8,128)S(1)}, u32[]{:S(2)}, u32[]{:S(2)}) %collective-permute-start.1) | collective-permute-done | bytes 122912 | tf_op jit(solution)/shard_map/ppermute | solution.py:682
  41.3 0.0 copy-done.1
  41.3 0.0 copy-done.2
  41.3 0.0 copy-done.3
  41.3 0.0 copy-done.4
  41.3 14.6 %pairs_density.1 = (f32[64,128]{1,0:T(8,128)}, f32[9,24,128]{2,1,0:T(8,128)S(1)}, s32[24,128]{1,0:T(8,128)S(1)}) custom-call(s32[2,16]{1,0:T(2,128)S(1)} %get-tuple-element.16.pairs_ref, f32[6,64,128]{2,1,0:T(8,128)S(1)} %get-tuple-element.17.stat_ref.core_ref.sorted_ref, f32[6,40,128]{2,1,0:T(8,128)S(1)} %collective-permute-done.lower_stat_ref.lower_ref, ...), custom_call_target="tpu_custom_call" | custom-call | flops 71303168 | bytes 2000000 | tf_op jit(solution)/shard_map/pairs_density/pallas_call | solution.py:494
  55.9 0.0 all-to-all-done
  55.9 1.3 %feed.1 = (f32[128,8]{1,0:T(8,128)}, f32[24,128]{1,0:T(8,128)S(1)}, s32[24,128]{1,0:T(8,128)S(1)}) custom-call(f32[9,24,128]{2,1,0:T(8,128)S(1)} %get-tuple-element.22.picked_ref, s32[24,128]{1,0:T(8,128)S(1)} %get-tuple-element.23.place_ref, s32[1,128]{1,0:T(1,128)S(1)} %get-tuple-element.24.count_ref, f32[1024,128]{1,0:T(8,128)S(1)} %bitcast.20), custom_call_target="tpu_custom_call" | custom-call | flops 1000000 | bytes 1000000 | tf_op jit(solution)/shard_map/feed/pallas_call | solution.py:577
  57.1 14.2 %all-to-all-start.1 = ((f32[128,1,8]{2,1,0:T(1,128)}), f32[128,1,8]{2,1,0:T(1,128)S(1)}, u32[]{:S(2)}, u32[]{:S(2)}) async-start(f32[128,1,8]{2,1,0:T(1,128)} %bitcast.14), calls=%async_computation.1 | async-start | bytes 131072 | tf_op jit(solution)/shard_map/all_to_all | solution.py:709
  71.4 1.8 %apply.1 = f32[2,64,128]{2,1,0:T(8,128)} custom-call(f32[24,128]{1,0:T(8,128)S(1)} %get-tuple-element.26.lost_ref, s32[24,128]{1,0:T(8,128)S(1)} %get-tuple-element.27.gas_at_ref, f32[5,64,128]{2,1,0:T(8,128)S(1)} %bitcast.23, f32[64,128]{1,0:T(8,128)S(1)} %bitcast.26), custom_call_target="tpu_custom_call" | custom-call | flops 1000000 | bytes 100000 | tf_op jit(solution)/shard_map/apply/pallas_call | solution.py:618
  73.2 9.7 %all-to-all-done.1 = f32[128,1,8]{2,1,0:T(1,128)S(1)} async-done(((f32[128,1,8]{2,1,0:T(1,128)}), f32[128,1,8]{2,1,0:T(1,128)S(1)}, u32[]{:S(2)}, u32[]{:S(2)}) %all-to-all-start.1) | async-done | bytes 4128 | tf_op jit(solution)/shard_map/all_to_all | solution.py:709
  82.9 0.7 settle.1
Async XLA Ops:
  0.6 0.7 copy-start.7
  0.6 0.7 copy-start.9
  0.7 0.7 copy-start.10
  0.7 0.7 copy-start.5
  0.7 0.7 copy-start.6
  0.7 0.7 copy-start.8
  2.2 24.6 %copy-start = (f32[5,1,1,8192]{3,2,1,0:T(1,128)S(1)}, f32[5,1,1,8192]{3,2,1,0:T(1,128)}, u32[]{:S(2)}) copy-start(f32[5,1,1,8192]{3,2,1,0:T(1,128)} %param.11) | copy-start | bytes 491524
  2.2 53.7 %all-to-all-start = ((f32[128,8,128]{2,1,0:T(8,128)}), f32[128,8,128]{2,1,0:T(8,128)S(1)}, u32[]{:S(2)}, u32[]{:S(2)}) async-start(f32[128,8,128]{2,1,0:T(8,128)} %get-tuple-element.25), calls=%async_computation | async-start | bytes 1048576 | tf_op jit(solution)/shard_map/all_to_all | solution.py:692
  28.6 11.7 %collective-permute-start = (f32[6,40,128]{2,1,0:T(8,128)S(1)}, f32[6,40,128]{2,1,0:T(8,128)S(1)}, u32[]{:S(2)}, u32[]{:S(2)}) collective-permute-start(f32[6,40,128]{2,1,0:T(8,128)S(1)} %get-tuple-element.18), channel_id=1, source_target_pairs={{0,1},{1,2},{2,3},{3,4},{4,5},{5,6},{6,7},{7,8},{8,9},{9,10},{10,1... | collective-permute-start | bytes 368648 | tf_op jit(solution)/shard_map/ppermute | solution.py:681
  30.2 11.0 %collective-permute-start.1 = (f32[6,40,128]{2,1,0:T(8,128)S(1)}, f32[6,40,128]{2,1,0:T(8,128)S(1)}, u32[]{:S(2)}, u32[]{:S(2)}) collective-permute-start(f32[6,40,128]{2,1,0:T(8,128)S(1)} %get-tuple-element.19), channel_id=1, source_target_pairs={{1,0},{2,1},{3,2},{4,3},{5,4},{6,5},{7,6},{8,7},{9,8},{10,9},{11,1... | collective-permute-start | bytes 368648 | tf_op jit(solution)/shard_map/ppermute | solution.py:682
  30.2 11.0 %copy-start.1 = (f32[1,1,8192]{2,1,0:T(1,128)S(1)}, f32[1,1,8192]{2,1,0:T(1,128)}, u32[]{:S(2)}) copy-start(f32[1,1,8192]{2,1,0:T(1,128)} %param.13) | copy-start | bytes 98308
  30.2 11.0 %copy-start.2 = (f32[3,1,1,8192]{3,2,1,0:T(1,128)S(1)}, f32[3,1,1,8192]{3,2,1,0:T(1,128)}, u32[]{:S(2)}) copy-start(f32[3,1,1,8192]{3,2,1,0:T(1,128)} %param.12) | copy-start | bytes 294916
  30.2 11.0 %copy-start.3 = (s32[1,1,3072]{2,1,0:T(1,128)S(1)}, s32[1,1,3072]{2,1,0:T(1,128)}, u32[]{:S(2)}) copy-start(s32[1,1,3072]{2,1,0:T(1,128)} %param.19) | copy-start | bytes 36868
  30.3 11.0 %copy-start.4 = (s32[1,1,3072]{2,1,0:T(1,128)S(1)}, s32[1,1,3072]{2,1,0:T(1,128)}, u32[]{:S(2)}) copy-start(s32[1,1,3072]{2,1,0:T(1,128)} %param.20) | copy-start | bytes 36868
  57.1 25.7 %all-to-all-start.1 = ((f32[128,1,8]{2,1,0:T(1,128)}), f32[128,1,8]{2,1,0:T(1,128)S(1)}, u32[]{:S(2)}, u32[]{:S(2)}) async-start(f32[128,1,8]{2,1,0:T(1,128)} %bitcast.14), calls=%async_computation.1 | async-start | bytes 131072 | tf_op jit(solution)/shard_map/all_to_all | solution.py:709
